TPU v7x, 32 devices: a whole 2x2x4 slice. The times are simulated.
32 devices in a mesh: tok: 4 (over z), col: 8 (over y, x, core).
Axes of the slice: x: 2, y: 2, z: 4, core: 2. Of those that a mesh axis runs over, the one named last changes fastest.
Arguments:
- activations: bfloat16 [1024, 4096], P('tok'), may hold values from -6 to 6
- out_grad: bfloat16 [1024, 8192], P('tok', 'col'), may hold values from -0.1875 to 0.1875
- owned_blocks: int32 [4, 8, 5], P('tok'), may hold values from -1 to 127, as said below
- gram_left: float32 [4, 8, 5, 512, 512], P('tok', 'col'), may hold values from -6144 to 6656, as said below
- gram_right: float32 [4, 8, 5, 512, 512], P('tok', 'col'), may hold values from -6144 to 6656, as said below
Outputs:
- precond: bfloat16 [4096, 8192], P('tok', 'col')
- left_new: float32 [4, 8, 5, 512, 512], P('tok', 'col')
- right_new: float32 [4, 8, 5, 512, 512], P('tok', 'col')
Inputs may be any that keep to these rules, and one draw needn't show every extreme that they name: owned_blocks[t] lists every block whose rows lie in rows t * 2 * 512 to (t + 1) * 2 * 512 - 1 exactly once; each device lists its block ids in ascending order followed by -1; the blocks of one device lie in pairwise different block columns; in each t some device fills all 5 slots. `gram_left`: each slot holds a symmetric positive definite matrix with eigenvalues of at least 256. `gram_right`: each slot holds a symmetric positive definite matrix with eigenvalues of at least 256.
All inputs are finite; a program needn't handle non-finite values.
Results may differ from a plain program's by a relative error of at most 0.015.
Values may be sent and summed in bfloat16 or wider, within the bound.
A program may use at most 128 MiB of HBM per device.

v0:
```python
import jax
import jax.numpy as jnp
from jax import lax
from jax.sharding import PartitionSpec as P

D = 8192
DI = 4096
B = 512
ITERS = 2


highest = lax.Precision.HIGHEST
decay_rate = 0.9
epsilon = 1e-06


def inverse_root(matrix):
    side = matrix.shape[-1]
    identity = jnp.eye(side, dtype=jnp.float32)
    mean_diag = jnp.trace(matrix, axis1=-2, axis2=-1) / side
    coupled = matrix / mean_diag[..., None, None]
    root = identity
    for iteration in range(ITERS):
        factor = (5.0 * identity - coupled) * 0.25
        if iteration == 0:
            root = factor
        else:
            root = jnp.einsum("...ij,...jk->...ik", root, factor, precision=highest)
        if iteration + 1 < ITERS:
            squared = jnp.einsum("...ij,...jk->...ik", factor, factor, precision=highest)
            fourth = jnp.einsum("...ij,...jk->...ik", squared, squared, precision=highest)
            coupled = jnp.einsum("...ij,...jk->...ik", fourth, coupled, precision=highest)
    return root


def per_device(activations, out_grad, owned_blocks, gram_left, gram_right):
    tok_count = lax.axis_size("tok")
    col_count = lax.axis_size("col")
    tok_index = lax.axis_index("tok")
    col_index = lax.axis_index("col")
    shard_width = out_grad.shape[1]
    rows_home = DI // tok_count
    row_blocks = rows_home // B
    col_blocks = D // B
    piece_width = min(B, shard_width)
    per_home = max(1, shard_width // B)
    per_block = B // piece_width
    owner_table = owned_blocks[0]
    slot_count = owner_table.shape[1]
    summed = lax.psum_scatter(
        lax.dot_general(
            activations, out_grad, (((0,), (0,)), ((), ())), preferred_element_type=jnp.float32
        ).astype(jnp.bfloat16),
        "tok",
        scatter_dimension=0,
        tiled=True,
    )
    home_pieces = summed.reshape(row_blocks, B, per_home, piece_width).transpose(0, 2, 1, 3)
    my_blocks = lax.dynamic_index_in_dim(owner_table, col_index, 0, keepdims=False)
    occupied = my_blocks >= 0
    clamped = jnp.where(occupied, my_blocks, 0)
    block_rows = jnp.clip(clamped // col_blocks - tok_index * row_blocks, 0, row_blocks - 1)
    block_cols = clamped % col_blocks
    piece_index = jnp.arange(per_block)
    first_column = block_cols[:, None] * B + piece_index[None, :] * piece_width
    sources = first_column // shard_width
    slices = first_column % shard_width // piece_width
    offsets = jnp.arange(per_home)
    initial = jnp.zeros((slot_count, per_block, B, piece_width), jnp.bfloat16)
    shard = lax.all_gather(home_pieces[None], "col", axis=0, tiled=True)
    first_index = jnp.int32(0)
    shard_count = shard.shape[0]
    inside = (sources >= first_index) & (sources < first_index + shard_count)
    local_index = jnp.clip(sources, 0, shard_count - 1)
    taken = shard[local_index, block_rows[:, None], slices]
    pieces = jnp.where(inside[:, :, None, None], taken, initial)
    blocks = pieces.transpose(0, 2, 1, 3).reshape(slot_count, B, B)
    gradient = jnp.where(occupied[:, None, None], blocks.astype(jnp.float32), jnp.float32(0.0))
    left_old = gram_left[0, 0]
    right_old = gram_right[0, 0]
    left_next = jnp.where(
        occupied[:, None, None],
        decay_rate * left_old + jnp.einsum("sij,skj->sik", gradient, gradient, precision=highest),
        left_old,
    )
    right_next = jnp.where(
        occupied[:, None, None],
        decay_rate * right_old + jnp.einsum("sji,sjk->sik", gradient, gradient, precision=highest),
        right_old,
    )
    root_left = inverse_root(left_next)
    root_right = inverse_root(right_next)
    shaped = jnp.einsum("sij,sjk->sik", root_left, gradient, precision=highest)
    shaped = jnp.einsum("sij,sjk->sik", shaped, root_right, precision=highest)
    grad_norm = jnp.sqrt(jnp.sum(gradient * gradient, axis=(1, 2)) + epsilon)
    shaped_norm = jnp.sqrt(jnp.sum(shaped * shaped, axis=(1, 2)) + epsilon)
    result = (shaped * (grad_norm / shaped_norm)[:, None, None]).astype(jnp.bfloat16)
    result_pieces = result.reshape(slot_count, B, per_block, piece_width).transpose(0, 2, 1, 3)
    home_ids = jnp.arange(col_count)
    global_cols = home_ids[:, None] * shard_width + offsets[None, :] * piece_width
    target_cols = global_cols // B
    matches_back = occupied[None, None, :] & (block_cols[None, None, :] == target_cols[:, :, None])
    present_back = jnp.any(matches_back, axis=2)
    slot_pick = jnp.sum(jnp.where(matches_back, jnp.arange(slot_count)[None, None, :], 0), axis=2)
    part_pick = global_cols % B // piece_width
    returning = result_pieces[slot_pick, part_pick]
    returning = jnp.where(present_back[:, :, None, None], returning, jnp.zeros((), jnp.bfloat16))
    arriving = lax.all_to_all(returning, "col", split_axis=0, concat_axis=0, tiled=True)
    wanted_home = (col_index * shard_width + offsets * piece_width) // B
    block_ids = (tok_index * row_blocks + jnp.arange(row_blocks))[
        :, None
    ] * col_blocks + wanted_home[None, :]
    owns_it = jnp.any(owner_table[None, None, :, :] == block_ids[:, :, None, None], axis=3)
    owner_ids = jnp.sum(jnp.where(owns_it, home_ids[None, None, :], 0), axis=2)
    gathered_home = arriving[owner_ids, offsets[None, :]]
    precond = gathered_home.transpose(0, 2, 1, 3).reshape(rows_home, shard_width)
    return (precond, left_next[None, None], right_next[None, None])


def solution(mesh):
    in_specs = (
        P("tok", None),
        P("tok", "col"),
        P("tok", None, None),
        P("tok", "col", None, None, None),
        P("tok", "col", None, None, None),
    )
    out_specs = (
        P("tok", "col"),
        P("tok", "col", None, None, None),
        P("tok", "col", None, None, None),
    )
    return jax.shard_map(
        per_device, mesh=mesh, in_specs=in_specs, out_specs=out_specs, check_vma=False
    )
```

profile of v0, /device:TPU:0, one launch (start us, length us, event | category | flops | bytes accessed | tf_op | source)
XLA Modules:
  0.0 531.9 jit_solution(12535325311539479131)
XLA Ops:
  7.2 1.5 copy-done
  8.8 6.7 %convolution_convert_fusion = bf16[4096,1024]{1,0:T(8,128)(2,1)} fusion(bf16[256,4096]{1,0:T(8,128)(2,1)S(1)} %copy-done, bf16[256,1024]{1,0:T(8,128)(2,1)} %param.6), kind=kOutput, calls=%fused_computation.4 | convolution fusion | flops 2151677952 | bytes 11010048 | tf_op jit(solution)/shard_map/dot_general | solution.py:51
  15.5 147.4 %reduce-scatter.2.cloned.1.call-done = bf16[1024,1024]{1,0:T(8,128)(2,1)} async-done(((bf16[4096,1024]{1,0:T(8,128)(2,1)}), bf16[1024,1024]{1,0:T(8,128)(2,1)}) %reduce-scatter.2.cloned.1.call-update) | async-done | bytes 2097168 | tf_op jit(solution)/shard_map/reduce_scatter | solution.py:50
  162.9 3.3 reshape.652
  166.2 1.7 copy.33
  167.9 0.3 compare_reduce_fusion.1
  168.2 0.4 fusion.32
  169.3 1.1 broadcast_select_fusion.2
  170.5 87.9 %all-gather.3.cloned.1.call-done = bf16[16,2,512,512]{3,2,1,0:T(8,128)(2,1)} async-done(((bf16[2,2,512,512]{3,2,1,0:T(8,128)(2,1)}), bf16[16,2,512,512]{3,2,1,0:T(8,128)(2,1)}) %all-gather.3.cloned.1.call-update) | async-done | bytes 16777232 | tf_op jit(solution)/shard_map/all_gather | solution.py:70
  258.4 6.5 %gather_fusion = bf16[5,512,512]{2,1,0:T(8,128)(2,1)S(1)} fusion(bf16[8,2,2,512,512]{4,3,2,1,0:T(8,128)(2,1)} %bitcast.75, s32[5]{0:T(128)S(1)} %or_bitcast_fusion), kind=kCustom, calls=%fused_computation | custom fusion | bytes 5242940 | tf_op jit(solution)/shard_map/gather | solution.py:75
  264.9 1.1 multiply_reduce_fusion.1
  266.0 15.4 %bitcast_select_fusion.1 = f32[5,512,512]{2,1,0:T(8,128)S(1)} fusion(f32[1,1,5,512,512]{4,3,2,1,0:T(8,128)} %param.8, pred[5]{0:T(512)(128)(4,1)S(1)} %get-tuple-element.8, bf16[5,512,512]{2,1,0:T(8,128)(2,1)S(1)} %gather_fusion, pred[5]{0:T(512)(128)(4,1)S(1)} %get-tuple-element.7), kind=kOutput, calls=%fused_computation.8 | convolution fusion | flops 8060928000 | bytes 13107210 | tf_op jit(solution)/shard_map/sij,skj->sik/dot_general | solution.py:83
  281.5 12.5 %select_reduce_fusion = (f32[5]{0:T(128)S(1)}, f32[5]{0:T(128)S(1)}, f32[5,512,512]{2,1,0:T(8,128)S(1)}) fusion(pred[512,512]{1,0:T(8,128)(4,1)S(1)} %iota_compare_fusion, f32[5,512,512]{2,1,0:T(8,128)S(1)} %bitcast_select_fusion.1, pred[5]{0:T(512)(128)(4,1)S(1)} %get-tuple-element.8, bf16[5,512,512]{2,1,0:T(8,128)(2,1)S(1)} %gather_fusion, ...), kind=kOutput, calls=%fused_computation.18 | convolution fusion | flops 8066170880 | bytes 18612274 | tf_op jit(solution)/shard_map/sji,sjk->sik/dot_general | solution.py:88
  294.0 2.4 copy-done.6
  296.4 10.5 %fusion.12 = f32[5,512,512]{2,1,0:T(8,128)S(1)} fusion(f32[512,512]{1,0:T(8,128)S(1)} %copy-done.2, f32[5,512,512]{2,1,0:T(8,128)S(1)} %get-tuple-element.12, f32[5]{0:T(128)S(1)} %get-tuple-element.15), kind=kOutput, calls=%fused_computation.29 | convolution fusion | flops 8056995840 | bytes 11534356 | tf_op jit(solution)/shard_map/...ij,...jk->...ik/dot_general | solution.py:30
  306.9 9.7 %fusion.56 = f32[5,512,512]{2,1,0:T(8,128)S(1)} fusion(f32[5,512,512]{2,1,0:T(8,128)S(1)} %fusion.12), kind=kOutput, calls=%fused_computation.146 | convolution fusion | flops 8053063680 | bytes 10485760 | tf_op jit(solution)/shard_map/...ij,...jk->...ik/dot_general | solution.py:31
  316.6 9.7 %fusion.54 = f32[5,512,512]{2,1,0:T(8,128)S(1)} fusion(f32[5,512,512]{2,1,0:T(8,128)S(1)} %fusion.56, f32[5,512,512]{2,1,0:T(8,128)S(1)} %copy-done.7, f32[5]{0:T(128)S(1)} %get-tuple-element.15), kind=kOutput, calls=%fused_computation.144 | convolution fusion | flops 8054374400 | bytes 15728660 | tf_op jit(solution)/shard_map/...ij,...jk->...ik/dot_general | solution.py:32
  326.3 9.9 %fusion.2 = f32[5,512,512]{2,1,0:T(8,128)S(1)} fusion(f32[5,512,512]{2,1,0:T(8,128)S(1)} %fusion.54, f32[512,512]{1,0:T(8,128)S(1)} %copy-done.2, f32[5,512,512]{2,1,0:T(8,128)S(1)} %copy-done.7, f32[5]{0:T(128)S(1)} %get-tuple-element.15), kind=kOutput, calls=%fused_computation.14 | convolution fusion | flops 8059617280 | bytes 16777236 | tf_op jit(solution)/shard_map/...ij,...jk->...ik/dot_general | solution.py:28
  336.3 10.6 %fusion.11 = f32[5,512,512]{2,1,0:T(8,128)S(1)} fusion(f32[512,512]{1,0:T(8,128)S(1)} %copy-done.2, f32[5,512,512]{2,1,0:T(8,128)S(1)} %bitcast_select_fusion.1, f32[5]{0:T(128)S(1)} %get-tuple-element.16), kind=kOutput, calls=%fused_computation.28 | convolution fusion | flops 8056995840 | bytes 11534356 | tf_op jit(solution)/shard_map/...ij,...jk->...ik/dot_general | solution.py:30
  346.9 9.4 %fusion.55 = f32[5,512,512]{2,1,0:T(8,128)S(1)} fusion(f32[5,512,512]{2,1,0:T(8,128)S(1)} %fusion.11), kind=kOutput, calls=%fused_computation.145 | convolution fusion | flops 8053063680 | bytes 10485760 | tf_op jit(solution)/shard_map/...ij,...jk->...ik/dot_general | solution.py:31
  356.3 11.3 %fusion.53 = f32[5,512,512]{2,1,0:T(8,128)} fusion(f32[5,512,512]{2,1,0:T(8,128)S(1)} %fusion.55, f32[5,512,512]{2,1,0:T(8,128)S(1)} %copy-done.5, f32[5]{0:T(128)S(1)} %get-tuple-element.16), kind=kOutput, calls=%fused_computation.143 | convolution fusion | flops 8054374400 | bytes 15728660 | tf_op jit(solution)/shard_map/...ij,...jk->...ik/dot_general | solution.py:32
  367.7 15.1 %fusion.5 = f32[5,512,512]{2,1,0:T(8,128)S(1)} fusion(f32[5,512,512]{2,1,0:T(8,128)} %fusion.53, f32[512,512]{1,0:T(8,128)S(1)} %copy-done.2, f32[5,512,512]{2,1,0:T(8,128)S(1)} %copy-done.5, f32[5]{0:T(128)S(1)} %get-tuple-element.16), kind=kOutput, calls=%fused_computation.19 | convolution fusion | flops 8059617280 | bytes 16777236 | tf_op jit(solution)/shard_map/...ij,...jk->...ik/dot_general | solution.py:28
  382.8 9.6 %fusion.9 = f32[5,512,512]{2,1,0:T(8,128)S(1)} fusion(f32[5,512,512]{2,1,0:T(8,128)S(1)} %fusion.5, pred[5]{0:T(512)(128)(4,1)S(1)} %get-tuple-element.8, bf16[5,512,512]{2,1,0:T(8,128)(2,1)S(1)} %gather_fusion, pred[5]{0:T(512)(128)(4,1)S(1)} %get-tuple-element.7), kind=kOutput, calls=%fused_computation.26 | convolution fusion | flops 8056995840 | bytes 13107210 | tf_op jit(solution)/shard_map/sij,sjk->sik/dot_general | solution.py:93
  392.4 9.6 %multiply_reduce_fusion = (f32[5]{0:T(128)S(1)}, f32[5,512,512]{2,1,0:T(8,128)S(1)}) fusion(f32[5,512,512]{2,1,0:T(8,128)S(1)} %fusion.9, f32[5,512,512]{2,1,0:T(8,128)S(1)} %fusion.2), kind=kOutput, calls=%fused_computation.12 | convolution fusion | flops 8055685120 | bytes 15728660 | tf_op jit(solution)/shard_map/sij,sjk->sik/dot_general | solution.py:94
  402.0 0.8 fusion.13
  402.8 4.6 gather_fusion.1
  407.4 7.2 %broadcast_select_fusion = bf16[8,2,512,512]{3,2,1,0:T(8,128)(2,1)} fusion(bf16[8,2,512,512]{3,2,1,0:T(8,128)(2,1)} %bitcast.70, pred[8,2]{1,0:T(8,128)(4,1)S(1)} %copy.23), kind=kLoop, calls=%fused_computation.3 | loop fusion | flops 4194304 | bytes 16777232 | tf_op jit(solution)/shard_map/jit(_where)/select_n | solution.py:107
  414.7 5.0 all-to-all-start
  420.3 93.4 %all-to-all-done = bf16[8,2,512,512]{3,2,1,0:T(8,128)(2,1)} async-done(((bf16[8,2,512,512]{3,2,1,0:T(8,128)(2,1)}), bf16[8,2,512,512]{3,2,1,0:T(8,128)(2,1)}, u32[]{:S(2)}, u32[]{:S(2)}) %all-to-all-start) | async-done | bytes 8388640 | tf_op jit(solution)/shard_map/all_to_all | solution.py:108
  513.7 5.5 %gather_fusion.2 = bf16[4,512,512]{2,1,0:T(8,128)(2,1)} fusion(bf16[8,2,512,512]{3,2,1,0:T(8,128)(2,1)} %all-to-all-done, s32[4]{0:T(128)S(1)} %reshape.668), kind=kCustom, calls=%fused_computation.2 | custom fusion | bytes 4194336 | tf_op jit(solution)/shard_map/gather | solution.py:115
  519.3 3.7 copy.28
  523.0 1.9 copy.31
  (46 shorter events, 1.6 us)
Async XLA Ops:
  7.2 1.6 copy-start
  7.2 155.7 %reduce-scatter.2.cloned.1.call-start = ((), (), s32[]{:S(2)}) async-start(), calls=%async_computation.2 | async-start | bytes 10485760 | tf_op jit(solution)/shard_map/reduce_scatter | solution.py:50
  15.4 152.5 %copy-start.3 = (s32[1,8,5]{1,0,2:T(1,128)S(1)}, s32[1,8,5]{1,0,2:T(1,128)}, u32[]{:S(2)}) copy-start(s32[1,8,5]{1,0,2:T(1,128)} %param.7) | copy-start | bytes 484
  15.5 243.0 %all-gather.3.cloned.1.call-start = ((), (), s32[]{:S(2)}) async-start(), calls=%async_computation.3 | async-start | bytes 18874368 | tf_op jit(solution)/shard_map/all_gather | solution.py:70
  264.9 16.5 %slice-start = ((s8[5242880]{0:T(1024)(128)(4,1)}), s8[4194304]{0:T(1024)(128)(4,1)S(1)}, s32[]{:S(2)}) async-start(s8[5242880]{0:T(1024)(128)(4,1)} %bitcast.77), calls=%async_computation.4 | async-start | bytes 8388608
  266.0 15.4 %slice-start.1 = ((s8[5242880]{0:T(1024)(128)(4,1)}), s8[1048576]{0:T(1024)(128)(4,1)S(1)}, s32[]{:S(2)}) async-start(s8[5242880]{0:T(1024)(128)(4,1)} %bitcast.77), calls=%async_computation.5 | async-start | bytes 2097152
  281.4 54.8 %copy-start.4 = (f32[5,512,512]{2,1,0:T(8,128)}, f32[5,512,512]{2,1,0:T(8,128)S(1)}, u32[]{:S(2)}) copy-start(f32[5,512,512]{2,1,0:T(8,128)S(1)} %bitcast_select_fusion.1) | copy-start | bytes 15728644
  281.4 14.9 %copy-start.2 = (f32[512,512]{1,0:T(8,128)S(1)}, f32[512,512]{1,0:T(8,128)}, u32[]{:S(2)}) copy-start(f32[512,512]{1,0:T(8,128)} %broadcast_select_fusion.2) | copy-start | bytes 3145732
  294.0 2.4 copy-start.6
  306.9 9.7 %copy-start.7 = (f32[5,512,512]{2,1,0:T(8,128)S(1)}, f32[5,512,512]{2,1,0:T(8,128)}, u32[]{:S(2)}) copy-start(f32[5,512,512]{2,1,0:T(8,128)} %copy-done.6) | copy-start | bytes 15728644
  346.9 9.4 %copy-start.5 = (f32[5,512,512]{2,1,0:T(8,128)S(1)}, f32[5,512,512]{2,1,0:T(8,128)}, u32[]{:S(2)}) copy-start(f32[5,512,512]{2,1,0:T(8,128)} %copy-done.4) | copy-start | bytes 15728644
  414.7 99.1 %all-to-all-start = ((bf16[8,2,512,512]{3,2,1,0:T(8,128)(2,1)}), bf16[8,2,512,512]{3,2,1,0:T(8,128)(2,1)}, u32[]{:S(2)}, u32[]{:S(2)}) async-start(bf16[8,2,512,512]{3,2,1,0:T(8,128)(2,1)} %broadcast_select_fusion), calls=%async_computation.1 | async-start | bytes 16777216 | tf_op jit(solution)/shard_map/all_to_all | solution.py:108
  513.7 11.2 %copy-start.1 = (bf16[256,4096]{1,0:T(8,128)(2,1)S(1)}, bf16[256,4096]{1,0:T(8,128)(2,1)}, u32[]{:S(2)}) copy-start(bf16[256,4096]{1,0:T(8,128)(2,1)} %param.5) | copy-start | bytes 6291460
Sparse Core Ops, SparseCore 0:
  15.6 147.3 reduce-scatter.1
  168.1 90.3 all-gather.2
where the time goes:
time: 540 us; the launch traced here: 532 us
  waiting for transfers between devices  329 us (61%)
  matrix products  140 us (26%)
  local copies, waits for them, and re-layouts  31.6 us (6%)
  between operations  14.5 us (3%)
  other arithmetic  11.9 us (2%)
    reduce_scatter x1, waiting for transfers between devices, per_device(): lax.psum_scatter(lax.dot_general(activations, out_grad, (((0,), (0,)), ((...  147 us
    all_to_all x1, waiting for transfers between devices, per_device(): lax.all_to_all(returning, 'col', split_axis=0, concat_axis=0, tiled=True)  93.4 us
    all_gather x1, waiting for transfers between devices, per_device(): shard = lax.all_gather(home_pieces[None], 'col', axis=0, tiled=True)  87.9 us
    dot_general x2, matrix products, inverse_root(): root = jnp.einsum('...ij,...jk->...ik', root, factor, precision=highest)  25 us
    dot_general x2, matrix products, inverse_root(): jnp.einsum('...ij,...jk->...ik', factor, factor, precision=highest)  21.1 us
    dot_general x2, matrix products, inverse_root(): jnp.einsum('...ij,...jk->...ik', fourth, coupled, precision=highest)  21 us
    dot_general x2, matrix products, inverse_root(): jnp.einsum('...ij,...jk->...ik', squared, squared, precision=highest)  19.1 us
    dot_general x1, matrix products, per_device(): jnp.einsum('sij,skj->sik', gradient, gradient, precision=highest)  15.4 us
  transfers between devices with their start and end apart: 3, of which 3 were waited for; matrix products, arithmetic and copies ran while one was open for 1% of the time, Pallas kernels for 0%

commit v1 on v0

v1 whole, which is shorter than its diff:
```python
import jax
import jax.numpy as jnp
from jax import lax
from jax.sharding import PartitionSpec as P

B = 512
decay_rate = 0.9
epsilon = 1e-06
f32 = jnp.float32
bf16 = jnp.bfloat16


def mm(a, b):
    return jnp.einsum("sij,sjk->sik", a.astype(bf16), b.astype(bf16), preferred_element_type=f32)


def root_minus_identity(matrix):
    side = matrix.shape[-1]
    identity = jnp.eye(side, dtype=f32)
    mean_diag = jnp.trace(matrix, axis1=-2, axis2=-1) / side
    e = (identity - matrix / mean_diag[..., None, None]) * 0.25
    w = 2.0 * e + mm(e, e)
    v = w + e + mm(e, w)
    r = v - 1.25 * w
    return 1.25 * e + r - 0.25 * v + mm(v, r)


def per_device(activations, out_grad, owned_blocks, gram_left, gram_right):
    tok_count = lax.axis_size("tok")
    col_count = lax.axis_size("col")
    tok_index = lax.axis_index("tok")
    col_index = lax.axis_index("col")
    tok_local, shard_width = out_grad.shape
    rows_home = activations.shape[1] // tok_count
    row_blocks = rows_home // B
    col_blocks = shard_width * col_count // B
    piece_width = min(B, shard_width)
    per_home = shard_width // piece_width
    per_block = B // piece_width
    sub = piece_width // col_count
    part = per_block * sub
    owners = owned_blocks[0]
    slots = owners.shape[1]

    og = out_grad.T.reshape(per_home, col_count, sub, tok_local).transpose(1, 0, 2, 3)
    og = lax.all_to_all(og, "col", split_axis=0, concat_axis=0, tiled=True)
    og = og.reshape(col_count * per_home * sub, tok_local)
    og = lax.all_gather(og, "tok", axis=1, tiled=True)
    act = lax.all_to_all(activations, "tok", split_axis=1, concat_axis=0, tiled=True)
    grad = jnp.dot(og, act, preferred_element_type=f32).astype(bf16)

    grad = grad.reshape(col_blocks, part, row_blocks, B)
    live = owners >= 0
    ids = jnp.where(live, owners, tok_index * row_blocks * col_blocks)
    send = grad[ids % col_blocks, :, ids // col_blocks - tok_index * row_blocks]
    got = lax.all_to_all(send, "col", split_axis=0, concat_axis=0, tiled=True)
    got = got.reshape(col_count, slots, per_block, sub, B).transpose(1, 2, 0, 3, 4)
    gt = got.reshape(slots, B, B)

    mine = lax.dynamic_index_in_dim(owners, col_index, 0, keepdims=False) >= 0
    mine = mine[:, None, None]
    gt = jnp.where(mine, gt, jnp.zeros((), bf16))
    left_old = gram_left[0, 0]
    right_old = gram_right[0, 0]
    left = jnp.einsum("sji,sjk->sik", gt, gt, preferred_element_type=f32)
    right = jnp.einsum("sij,skj->sik", gt, gt, preferred_element_type=f32)
    left_next = jnp.where(mine, decay_rate * left_old + left, left_old)
    right_next = jnp.where(mine, decay_rate * right_old + right, right_old)
    yl = root_minus_identity(left_next)
    yr = root_minus_identity(right_next)
    g32 = gt.astype(f32)
    first = g32 + mm(yr, gt)
    shaped = first + mm(first, yl)
    grad_norm = jnp.sqrt(jnp.sum(g32 * g32, axis=(1, 2)) + epsilon)
    shaped_norm = jnp.sqrt(jnp.sum(shaped * shaped, axis=(1, 2)) + epsilon)
    result = (shaped * (grad_norm / shaped_norm)[:, None, None]).astype(bf16)

    back = result.reshape(slots, per_block, col_count, sub, B).transpose(2, 0, 1, 3, 4)
    back = back.reshape(col_count, slots, part, B)
    back = lax.all_to_all(back, "col", split_axis=0, concat_axis=0, tiled=True)
    back = back.reshape(col_count * slots, per_block, sub, B)
    home = jnp.arange(col_count * per_home)
    wanted = (tok_index * row_blocks + jnp.arange(row_blocks))[None, :] * col_blocks + (
        home // per_block
    )[:, None]
    match = owners.reshape(-1)[None, None, :] == wanted[:, :, None]
    pick = jnp.argmax(match, axis=2)
    out = back[pick, (home % per_block)[:, None]]
    out = out.reshape(col_count, per_home, row_blocks, sub, B)
    out = lax.all_to_all(out, "col", split_axis=0, concat_axis=0, tiled=True)
    out = out.transpose(2, 4, 1, 0, 3).reshape(rows_home, shard_width)
    return (out, left_next[None, None], right_next[None, None])


def solution(mesh):
    in_specs = (
        P("tok", None),
        P("tok", "col"),
        P("tok", None, None),
        P("tok", "col", None, None, None),
        P("tok", "col", None, None, None),
    )
    out_specs = (
        P("tok", "col"),
        P("tok", "col", None, None, None),
        P("tok", "col", None, None, None),
    )
    return jax.shard_map(
        per_device, mesh=mesh, in_specs=in_specs, out_specs=out_specs, check_vma=False
    )
```

time: 540 us -> 345 us (0.64); the launches traced: 532 us -> 344 us
  waiting for transfers between devices: 329 us -> 147 us
  matrix products: 140 us -> 92.2 us
  blocking collectives: 0 us -> 30.1 us
  starting transfers between devices: 5.12 us -> 18.4 us
    reduce_scatter x1 -> x0, waiting for transfers between devices: 147 us -> none  [per_device(): lax.psum_scatter(lax.dot_general(activations, out_grad, (((0,), (0,)), ((...]
    all_gather x1, waiting for transfers between devices: 87.9 us -> 0.01 us  [per_device(): og = lax.all_gather(og, 'tok', axis=1, tiled=True)]
    all_to_all x1 -> x4, waiting for transfers between devices: 93.4 us -> 146 us  [the longest x1 78.7 us: per_device(): lax.all_to_all(activations, 'tok', split_axis=1, concat_axis=0, tiled=True)]
    dot_general x13 -> x9, matrix products: 140 us -> 92.2 us  [the longest x6 76.8 us: mm(): jnp.einsum('sij,sjk->sik', a.astype(bf16), b.astype(bf16), preferred_elem...]
    all_to_all x0 -> x1, blocking collectives: none -> 30.1 us  [per_device(): out = lax.all_to_all(out, 'col', split_axis=0, concat_axis=0, tiled=True)]
    gather x4 -> x2, local copies, waits for them, and re-layouts: 20.4 us -> 4.35 us  [the longest x1 2.36 us: per_device(): send = grad[ids % col_blocks, :, ids // col_blocks - tok_index * row_blocks]]
    unnamed x22 -> x25, local copies, waits for them, and re-layouts: 5.92 us -> 21.4 us
    all_to_all x1 -> x4, starting transfers between devices: 5.04 us -> 18.4 us  [the longest x1 5.33 us: per_device(): og = lax.all_to_all(og, 'col', split_axis=0, concat_axis=0, tiled=True)]
  transfers between devices with their start and end apart: 3 -> 5, of which waited for: 3 -> 4; matrix products, arithmetic and copies ran while one was open for 1% -> 3% of each run, Pallas kernels for 0% -> 0%
where the time goes in v1:
time: 345 us; the launch traced here: 344 us
  waiting for transfers between devices  147 us (43%)
  matrix products  92.2 us (27%)
  local copies, waits for them, and re-layouts  36 us (10%)
  blocking collectives  30.1 us (9%)
  starting transfers between devices  18.4 us (5%)
  between operations  14.2 us (4%)
  other arithmetic  6.52 us (2%)
    all_to_all x1, waiting for transfers between devices, per_device(): lax.all_to_all(activations, 'tok', split_axis=1, concat_axis=0, tiled=True)  78.7 us
    dot_general x6, matrix products, mm(): jnp.einsum('sij,sjk->sik', a.astype(bf16), b.astype(bf16), preferred_elem...  76.8 us
    all_to_all x1, waiting for transfers between devices, per_device(): back = lax.all_to_all(back, 'col', split_axis=0, concat_axis=0, tiled=True)  31 us
    all_to_all x1, waiting for transfers between devices, per_device(): got = lax.all_to_all(send, 'col', split_axis=0, concat_axis=0, tiled=True)  30.8 us
    all_to_all x1, blocking collectives, per_device(): out = lax.all_to_all(out, 'col', split_axis=0, concat_axis=0, tiled=True)  30.1 us
    unnamed x25, local copies, waits for them, and re-layouts  21.4 us
  transfers between devices with their start and end apart: 5, of which 4 were waited for; matrix products, arithmetic and copies ran while one was open for 3% of the time, Pallas kernels for 0%

profile of v1, /device:TPU:0, one launch (start us, length us, event | category | flops | bytes accessed | tf_op | source)
XLA Modules:
  0.0 344.3 jit_solution(13801665889047492123)
XLA Ops:
  7.2 1.2 copy.46
  9.2 5.3 %all-to-all-start = ((bf16[8,2,64,256]{3,2,1,0:T(8,128)(2,1)}), bf16[8,2,64,256]{3,2,1,0:T(8,128)(2,1)S(1)}, u32[]{:S(2)}, u32[]{:S(2)}) async-start(bf16[8,2,64,256]{3,2,1,0:T(8,128)(2,1)} %copy.47), calls=%async_computation | async-start | bytes 1048576 | tf_op jit(solution)/shard_map/all_to_all | solution.py:46
  14.6 4.1 %copy.48 = bf16[256,4096]{0,1:T(8,128)(2,1)} copy(bf16[256,4096]{1,0:T(8,128)(2,1)} %param.5) | data formatting | bytes 4194304 | tf_op args[0]
  18.6 5.6 %all-to-all-done = bf16[8,2,64,256]{3,2,1,0:T(8,128)(2,1)S(1)} async-done(((bf16[8,2,64,256]{3,2,1,0:T(8,128)(2,1)}), bf16[8,2,64,256]{3,2,1,0:T(8,128)(2,1)S(1)}, u32[]{:S(2)}, u32[]{:S(2)}) %all-to-all-start) | async-done | bytes 524320 | tf_op jit(solution)/shard_map/all_to_all | solution.py:46
  24.3 4.9 %all-to-all-start.1 = ((bf16[256,4,1024]{0,2,1:T(8,128)(2,1)}), bf16[256,4,1024]{0,2,1:T(8,128)(2,1)S(1)}, u32[]{:S(2)}, u32[]{:S(2)}) async-start(bf16[256,4,1024]{0,2,1:T(8,128)(2,1)} %bitcast.4), calls=%async_computation.1 | async-start | bytes 4194304 | tf_op jit(solution)/shard_map/all_to_all | solution.py:49
  30.1 78.7 %all-to-all-done.1 = bf16[256,4,1024]{0,2,1:T(8,128)(2,1)S(1)} async-done(((bf16[256,4,1024]{0,2,1:T(8,128)(2,1)}), bf16[256,4,1024]{0,2,1:T(8,128)(2,1)S(1)}, u32[]{:S(2)}, u32[]{:S(2)}) %all-to-all-start.1) | async-done | bytes 2097184 | tf_op jit(solution)/shard_map/all_to_all | solution.py:49
  108.8 2.4 copy.49
  111.2 4.5 %convolution_convert_fusion = bf16[1024,1024]{1,0:T(8,128)(2,1)S(1)} fusion(bf16[1024,1024]{1,0:T(8,128)(2,1)} %all-gather.2.cloned.1.call-done, bf16[1024,1024]{1,0:T(8,128)(2,1)} %bitcast.61), kind=kOutput, calls=%fused_computation.54 | convolution fusion | flops 2148532224 | bytes 6291456 | tf_op jit(solution)/shard_map/dot_general | solution.py:50
  115.7 2.8 reshape.219
  118.5 2.0 copy.51
  120.5 2.4 gather_fusion
  122.9 4.5 %all-to-all-start.2 = ((bf16[8,5,64,512]{3,2,1,0:T(8,128)(2,1)}), bf16[8,5,64,512]{3,2,1,0:T(8,128)(2,1)S(1)}, u32[]{:S(2)}, u32[]{:S(2)}) async-start(bf16[8,5,64,512]{3,2,1,0:T(8,128)(2,1)} %bitcast.51), calls=%async_computation.2 | async-start | bytes 5242880 | tf_op jit(solution)/shard_map/all_to_all | solution.py:56
  127.8 1.1 fusion.51
  128.9 30.8 %all-to-all-done.2 = bf16[8,5,64,512]{3,2,1,0:T(8,128)(2,1)S(1)} async-done(((bf16[8,5,64,512]{3,2,1,0:T(8,128)(2,1)}), bf16[8,5,64,512]{3,2,1,0:T(8,128)(2,1)S(1)}, u32[]{:S(2)}, u32[]{:S(2)}) %all-to-all-start.2) | async-done | bytes 2621472 | tf_op jit(solution)/shard_map/all_to_all | solution.py:56
  159.9 5.4 %bitcast_select_fusion.1 = f32[5,512,512]{2,1,0:T(8,128)S(1)} fusion(f32[1,1,5,512,512]{4,3,2,1,0:T(8,128)} %param.9, pred[5]{0:T(512)(128)(4,1)S(1)} %compare_reduce_fusion, bf16[5,512,512]{2,1,0:T(8,128)(2,1)S(1)} %bitcast.57), kind=kOutput, calls=%fused_computation.5 | convolution fusion | flops 1347420160 | bytes 13107205 | tf_op jit(solution)/shard_map/sij,skj->sik/dot_general | solution.py:66
  165.3 5.4 %select_reduce_fusion = (f32[5]{0:T(128)S(1)}, f32[5]{0:T(128)S(1)}, f32[5,512,512]{2,1,0:T(8,128)}) fusion(pred[512,512]{1,0:T(8,128)(4,1)S(1)} %iota_compare_fusion, f32[5,512,512]{2,1,0:T(8,128)S(1)} %bitcast_select_fusion.1, bf16[5,512,512]{2,1,0:T(8,128)(2,1)S(1)} %bitcast.58, pred[5]{0:T(512)(128)(4,1)S(1)} %compare_reduce_fusion, ...), kind=kOutput, calls=%fused_computation.16 | convolution fusion | flops 1352663040 | bytes 18612268 | tf_op jit(solution)/shard_map/sji,sjk->sik/dot_general | solution.py:65
  170.7 1.9 fusion.41
  172.7 2.4 copy-done.7
  175.0 4.5 %fusion.26 = f32[5,512,512]{2,1,0:T(8,128)} fusion(f32[5,512,512]{2,1,0:T(8,128)S(1)} %fusion.41, f32[5,512,512]{2,1,0:T(8,128)S(1)} %bitcast_select_fusion.1, f32[5]{0:T(128)S(1)} %get-tuple-element.23, f32[512,512]{1,0:T(8,128)S(1)} %copy-done.2), kind=kOutput, calls=%fused_computation.38 | convolution fusion | flops 1353973760 | bytes 16777236 | tf_op jit(solution)/shard_map/sij,sjk->sik/dot_general | solution.py:14
  179.6 25.6 %fusion.38 = f32[5,512,512]{2,1,0:T(8,128)} fusion(f32[5,512,512]{2,1,0:T(8,128)} %fusion.26, f32[5,512,512]{2,1,0:T(8,128)} %copy-done.7, bf16[5,512,512]{2,1,0:T(8,128)(2,1)} %bitcast.59, pred[5]{0:T(512)(128)(4,1)S(1)} %compare_reduce_fusion, f32[5,512,512]{2,1,0:T(8,128)} %copy-done.5, f32[5]{0:T(128)S(1)} %get-tuple-element.23, f32[512,512]{1,0:T(8,128)} %fusion.51), kind=kOutput, calls=%fused_computation.44 | convolution fusion | flops 2728919040 | bytes 24641560 | tf_op jit(solution)/shard_map/sij,sjk->sik/dot_general | solution.py:14
  205.2 6.5 %fusion.42 = f32[5,512,512]{2,1,0:T(8,128)S(1)} fusion(f32[5,512,512]{2,1,0:T(8,128)} %get-tuple-element.19, f32[5]{0:T(128)S(1)} %get-tuple-element.22, f32[512,512]{1,0:T(8,128)} %fusion.51), kind=kOutput, calls=%fused_computation.46 | convolution fusion | flops 1347420160 | bytes 11534356 | tf_op jit(solution)/shard_map/sij,sjk->sik/dot_general | solution.py:14
  211.7 2.4 copy-done.6
  214.0 8.7 %fusion.17 = f32[5,512,512]{2,1,0:T(8,128)} fusion(f32[5,512,512]{2,1,0:T(8,128)S(1)} %fusion.42, f32[5,512,512]{2,1,0:T(8,128)} %get-tuple-element.19, f32[5]{0:T(128)S(1)} %get-tuple-element.22, f32[512,512]{1,0:T(8,128)S(1)} %copy-done.3), kind=kOutput, calls=%fused_computation.34 | convolution fusion | flops 1353973760 | bytes 16777236 | tf_op jit(solution)/shard_map/sij,sjk->sik/dot_general | solution.py:14
  222.8 29.6 %multiply_reduce_fusion = (f32[5]{0:T(128)S(1)}, f32[5,512,512]{2,1,0:T(8,128)}) fusion(f32[5,512,512]{2,1,0:T(8,128)} %fusion.17, f32[5,512,512]{2,1,0:T(8,128)} %copy-done.6, f32[5,512,512]{2,1,0:T(8,128)} %get-tuple-element.19, f32[5]{0:T(128)S(1)} %get-tuple-element.22, f32[512,512]{1,0:T(8,128)} %fusion.51, f32[5,512,512]{2,1,0:T(8,128)} %fusion.38, ...), kind=kOutput, calls=%fused_computation.9 | convolution fusion | flops 2740715520 | bytes 29884460 | tf_op jit(solution)/shard_map/sij,sjk->sik/dot_general | solution.py:14
  253.3 3.3 multiply_convert_fusion
  256.6 1.7 copy.63
  258.3 3.6 %all-to-all-start.3 = ((bf16[8,5,64,512]{3,2,1,0:T(8,128)(2,1)}), bf16[8,5,64,512]{3,2,1,0:T(8,128)(2,1)S(1)}, u32[]{:S(2)}, u32[]{:S(2)}) async-start(bf16[8,5,64,512]{3,2,1,0:T(8,128)(2,1)} %bitcast.49), calls=%async_computation.3 | async-start | bytes 5242880 | tf_op jit(solution)/shard_map/all_to_all | solution.py:80
  263.1 31.0 %all-to-all-done.3 = bf16[8,5,64,512]{3,2,1,0:T(8,128)(2,1)S(1)} async-done(((bf16[8,5,64,512]{3,2,1,0:T(8,128)(2,1)}), bf16[8,5,64,512]{3,2,1,0:T(8,128)(2,1)S(1)}, u32[]{:S(2)}, u32[]{:S(2)}) %all-to-all-start.3) | async-done | bytes 2621472 | tf_op jit(solution)/shard_map/all_to_all | solution.py:80
  294.1 2.0 gather_fusion.1
  296.1 30.1 %all_to_all.39 = bf16[8,2,2,64,512]{4,3,2,1,0:T(8,128)(2,1)S(1)} all-to-all(bf16[8,2,2,64,512]{4,3,2,1,0:T(8,128)(2,1)} %bitcast.56), channel_id=1, replica_groups=mesh['tok'=4,'col'=8] {'col'}, dimensions={0} | all-to-all | bytes 4194304 | tf_op jit(solution)/shard_map/all_to_all | solution.py:90
  326.1 4.8 %copy.60 = bf16[2,512,2,8,64]{4,3,2,1,0:T(8,128)(2,1)} copy(bf16[2,512,2,8,64]{1,4,0,2,3:T(8,128)(2,1)S(1)} %bitcast.54) | data formatting | bytes 4194304
  330.9 6.5 %reshape.246 = bf16[1024,1024]{1,0:T(8,128)(2,1)} reshape(bf16[2,512,2,8,64]{4,3,2,1,0:T(8,128)(2,1)} %copy.60) | data formatting | bytes 4194304
  (40 shorter events, 4.4 us)
Async XLA Ops:
  9.2 20.6 %copy-start.4 = (s32[1,8,5]{1,0,2:T(1,128)S(1)}, s32[1,8,5]{1,0,2:T(1,128)}, u32[]{:S(2)}) copy-start(s32[1,8,5]{1,0,2:T(1,128)} %param.7) | copy-start | bytes 484
  9.2 15.0 %all-to-all-start = ((bf16[8,2,64,256]{3,2,1,0:T(8,128)(2,1)}), bf16[8,2,64,256]{3,2,1,0:T(8,128)(2,1)S(1)}, u32[]{:S(2)}, u32[]{:S(2)}) async-start(bf16[8,2,64,256]{3,2,1,0:T(8,128)(2,1)} %copy.47), calls=%async_computation | async-start | bytes 1048576 | tf_op jit(solution)/shard_map/all_to_all | solution.py:46
  24.3 4.9 %copy-start.1 = (bf16[8,2,64,256]{3,2,1,0:T(8,128)(2,1)}, bf16[8,2,64,256]{3,2,1,0:T(8,128)(2,1)S(1)}, u32[]{:S(2)}) copy-start(bf16[8,2,64,256]{3,2,1,0:T(8,128)(2,1)S(1)} %all-to-all-done) | copy-start | bytes 1572868
  24.3 84.5 %all-to-all-start.1 = ((bf16[256,4,1024]{0,2,1:T(8,128)(2,1)}), bf16[256,4,1024]{0,2,1:T(8,128)(2,1)S(1)}, u32[]{:S(2)}, u32[]{:S(2)}) async-start(bf16[256,4,1024]{0,2,1:T(8,128)(2,1)} %bitcast.4), calls=%async_computation.1 | async-start | bytes 4194304 | tf_op jit(solution)/shard_map/all_to_all | solution.py:49
  29.2 82.0 %all-gather.2.cloned.1.call-start = ((), (), s32[]{:S(2)}) async-start(), calls=%async_computation.5 | async-start | bytes 2621440 | tf_op jit(solution)/shard_map/all_gather | solution.py:48
  122.9 36.8 %all-to-all-start.2 = ((bf16[8,5,64,512]{3,2,1,0:T(8,128)(2,1)}), bf16[8,5,64,512]{3,2,1,0:T(8,128)(2,1)S(1)}, u32[]{:S(2)}, u32[]{:S(2)}) async-start(bf16[8,5,64,512]{3,2,1,0:T(8,128)(2,1)} %bitcast.51), calls=%async_computation.2 | async-start | bytes 5242880 | tf_op jit(solution)/shard_map/all_to_all | solution.py:56
  159.7 5.6 %slice-start = ((s8[5242880]{0:T(1024)(128)(4,1)}), s8[4194304]{0:T(1024)(128)(4,1)S(1)}, s32[]{:S(2)}) async-start(s8[5242880]{0:T(1024)(128)(4,1)} %bitcast.64), calls=%async_computation.6 | async-start | bytes 8388608
  159.8 5.4 %copy-start = (bf16[5,1,8,64,512]{4,3,2,0,1:T(8,128)(2,1)}, bf16[5,1,8,64,512]{4,3,2,0,1:T(8,128)(2,1)S(1)}, u32[]{:S(2)}) copy-start(bf16[5,1,8,64,512]{4,3,2,0,1:T(8,128)(2,1)S(1)} %copy.52) | copy-start | bytes 7864324
  159.8 5.4 %slice-start.1 = ((s8[5242880]{0:T(1024)(128)(4,1)}), s8[1048576]{0:T(1024)(128)(4,1)S(1)}, s32[]{:S(2)}) async-start(s8[5242880]{0:T(1024)(128)(4,1)} %bitcast.64), calls=%async_computation.7 | async-start | bytes 2097152
  165.3 7.4 %copy-start.5 = (f32[5,512,512]{2,1,0:T(8,128)}, f32[5,512,512]{2,1,0:T(8,128)S(1)}, u32[]{:S(2)}) copy-start(f32[5,512,512]{2,1,0:T(8,128)S(1)} %bitcast_select_fusion.1) | copy-start | bytes 15728644
  165.3 5.4 %copy-start.2 = (f32[512,512]{1,0:T(8,128)S(1)}, f32[512,512]{1,0:T(8,128)}, u32[]{:S(2)}) copy-start(f32[512,512]{1,0:T(8,128)} %fusion.51) | copy-start | bytes 3145732
  172.7 2.4 copy-start.7
  205.2 8.8 %copy-start.3 = (f32[512,512]{1,0:T(8,128)S(1)}, f32[512,512]{1,0:T(8,128)}, u32[]{:S(2)}) copy-start(f32[512,512]{1,0:T(8,128)} %fusion.51) | copy-start | bytes 3145732
  211.7 2.4 copy-start.6
  258.3 35.8 %all-to-all-start.3 = ((bf16[8,5,64,512]{3,2,1,0:T(8,128)(2,1)}), bf16[8,5,64,512]{3,2,1,0:T(8,128)(2,1)S(1)}, u32[]{:S(2)}, u32[]{:S(2)}) async-start(bf16[8,5,64,512]{3,2,1,0:T(8,128)(2,1)} %bitcast.49), calls=%async_computation.3 | async-start | bytes 5242880 | tf_op jit(solution)/shard_map/all_to_all | solution.py:80
Sparse Core Ops, SparseCore 0:
  32.1 76.6 all-gather.1

commit v2 on v1

v2 whole, which is shorter than its diff:
```python
import functools

import jax
import jax.numpy as jnp
from jax import lax
from jax.experimental import pallas as pl
from jax.experimental.pallas import tpu as pltpu
from jax.sharding import PartitionSpec as P

B = 512
decay_rate = 0.9
epsilon = 1e-06
f32 = jnp.float32
bf16 = jnp.bfloat16
MESH = pl.DeviceIdType.MESH
VMEM = pl.BlockSpec(memory_space=pltpu.VMEM)
ANY = pl.BlockSpec(memory_space=pl.ANY)
LIMIT = 60 * 1024 * 1024


def mm(a, b):
    return jnp.dot(a.astype(bf16), b.astype(bf16), preferred_element_type=f32)


def gather_kernel(tok_count, col_count, og_ref, act_ref, og_buf, act_buf, sems, local_sems):
    t = lax.axis_index("tok")
    c = lax.axis_index("col")
    core = lax.rem(c, 2)
    chip = c // 2
    chips = col_count // 2
    partner = chip * 2 + 1 - core
    width = act_buf.shape[3]

    barrier = pltpu.get_barrier_semaphore()
    for d in range(1, col_count):
        pl.semaphore_signal(
            barrier, inc=1, device_id=(t, lax.rem(c + d, col_count)), device_id_type=MESH
        )
    for d in range(1, tok_count):
        pl.semaphore_signal(
            barrier, inc=1, device_id=(lax.rem(t + d, tok_count), c), device_id_type=MESH
        )

    def act_piece(to):
        return act_ref.at[c, :, pl.ds(pl.multiple_of(to * width, width), width)]

    own_act = pltpu.make_async_copy(act_piece(t), act_buf.at[t, c], local_sems.at[0])
    own_act.start()
    own_og = pltpu.make_async_copy(og_ref.at[c], og_buf.at[t, c], local_sems.at[1])
    own_og.start()
    pl.semaphore_wait(barrier, col_count + tok_count - 2)

    def remote(src, dst, kind, sent, received, to):
        return pltpu.make_async_remote_copy(
            src_ref=src,
            dst_ref=dst,
            send_sem=sems.at[kind, 0, sent],
            recv_sem=sems.at[kind, 1, received],
            device_id=to,
            device_id_type=MESH,
        )

    sent = []
    for d in range(1, tok_count):
        to = lax.rem(t + d, tok_count)
        copy = remote(act_piece(to), act_buf.at[t, c], 0, d, t, (to, c))
        copy.start()
        sent.append(copy)
    for d in range(1, col_count):
        to = lax.rem(c + d, col_count)
        copy = remote(og_ref.at[to], og_buf.at[t, c], 1, d, c, (t, to))
        copy.start()
        sent.append(copy)

    for d in range(1, col_count):
        source = lax.rem(c + d, col_count)
        remote(og_buf.at[t, source], og_buf.at[t, source], 1, d, source, (t, source)).wait_recv()
    own_og.wait()

    def pass_on(origin, step, kind):
        to = t + step
        return remote(og_buf.at[origin], og_buf.at[origin], kind, origin, origin, (to, c))

    @pl.when(t < tok_count - 1)
    def _():
        pass_on(t, 1, 2).start()

    @pl.when(t > 0)
    def _():
        pass_on(t, -1, 3).start()

    own_act.wait()
    for d in range(1, tok_count):
        source = lax.rem(t + d, tok_count)
        remote(act_buf.at[source, c], act_buf.at[source, c], 0, d, source, (source, c)).wait_recv()

    def share(piece, kind, sem_sent, sem_received, to):
        return remote(
            act_buf.at[:, piece], act_buf.at[:, piece], kind, sem_sent, sem_received, (t, to)
        )

    for d in range(1, chips):
        to = lax.rem(chip + d, chips) * 2 + core
        copy = share(c, 4, d, chip, to)
        copy.start()
        sent.append(copy)
    copy = share(c, 5, 0, chip, partner)
    copy.start()
    sent.append(copy)

    def relay(origin, step, kind):
        pass_on(origin, -step, kind).wait_recv()

        @pl.when((t + step >= 0) & (t + step < tok_count))
        def _():
            pass_on(origin, step, kind).start()

    for d in range(1, chips):
        other = lax.rem(chip + d, chips)
        piece = other * 2 + core
        share(piece, 4, d, other, piece).wait_recv()
        copy = share(piece, 5, d, other, partner)
        copy.start()
        sent.append(copy)

    for d in range(1, tok_count):

        @pl.when(t - d >= 0)
        def _():
            relay(t - d, 1, 2)

        @pl.when(t + d < tok_count)
        def _():
            relay(t + d, -1, 3)

    for d in range(chips):
        other = lax.rem(chip + d, chips)
        piece = other * 2 + 1 - core
        share(piece, 5, d, other, partner).wait_recv()
    for copy in sent:
        copy.wait_send()
    for origin in range(tok_count):

        @pl.when((t >= origin) & (t < tok_count - 1))
        def _():
            pass_on(origin, 1, 2).wait_send()

        @pl.when((t <= origin) & (t > 0))
        def _():
            pass_on(origin, -1, 3).wait_send()


def grad_kernel(table, og_ref, act_ref, send_ref, grad, *, slots, row_blocks, col_count):
    tok_count = og_ref.shape[0]
    col_blocks, part = grad.shape[1:3]
    base = lax.axis_index("tok") * (row_blocks * col_blocks)
    step = 256
    blocks = step // part

    @pl.loop(0, col_blocks // blocks)
    def _(i):
        rows = pl.ds(pl.multiple_of(i * step, step), step)
        total = sum(
            jnp.dot(og_ref[t, rows], act_ref[t], preferred_element_type=f32)
            for t in range(tok_count)
        ).astype(bf16)
        for r in range(row_blocks):
            grad[r, pl.ds(i * blocks, blocks)] = total[:, r * B : (r + 1) * B].reshape(
                blocks, part, B
            )

    @pl.loop(0, col_count)
    def _(o):
        for s in range(slots):
            place = jnp.maximum(table[o * slots + s] - base, 0)
            send_ref[o, s] = grad[place // col_blocks, lax.rem(place, col_blocks)]


def root_minus_identity(matrix, diagonal):
    side = matrix.shape[-1]
    scale = 0.25 * side / jnp.sum(jnp.where(diagonal, matrix, 0.0))
    e = jnp.where(diagonal, 0.25, 0.0) - matrix * scale
    eb = e.astype(bf16)
    w = 2.0 * e + mm(eb, eb)
    v = w + e + mm(eb, w)
    r = v - 1.25 * w
    return (1.25 * e + r - 0.25 * v + mm(v, r)).astype(bf16)


def slot_kernel(live_ref, got_ref, left_ref, right_ref, back_ref, left_out, right_out):
    live = live_ref[pl.program_id(0)] > 0
    gt = got_ref[...].reshape(B, B)
    gt = jnp.where(live, gt, jnp.zeros_like(gt))
    g = gt.T
    rows = lax.broadcasted_iota(jnp.int32, (B, B), 0)
    cols = lax.broadcasted_iota(jnp.int32, (B, B), 1)
    diagonal = rows == cols
    decay = jnp.where(live, decay_rate, 1.0)
    left = decay * left_ref[0] + jnp.dot(g, gt, preferred_element_type=f32)
    right = decay * right_ref[0] + jnp.dot(gt, g, preferred_element_type=f32)
    left_out[0] = left
    right_out[0] = right
    yl = root_minus_identity(left, diagonal)
    yr = root_minus_identity(right, diagonal)
    g32 = gt.astype(f32)
    first = g32 + jnp.dot(yr, gt, preferred_element_type=f32)
    shaped = first + mm(first, yl)
    grad_norm = jnp.sqrt(jnp.sum(g32 * g32, keepdims=True) + epsilon)
    shaped_norm = jnp.sqrt(jnp.sum(shaped * shaped, keepdims=True) + epsilon)
    result = (shaped * (grad_norm / shaped_norm)).astype(bf16)
    back_ref[...] = result.reshape(back_ref.shape)


def place_kernel(in_ref, out_ref):
    width = out_ref.shape[1]
    out_ref[...] = in_ref[...].reshape(width, B).T


def per_device(activations, out_grad, owned_blocks, gram_left, gram_right):
    tok_count = lax.axis_size("tok")
    col_count = lax.axis_size("col")
    tok_index = lax.axis_index("tok")
    col_index = lax.axis_index("col")
    tok_local, shard_width = out_grad.shape
    rows_home = activations.shape[1] // tok_count
    row_blocks = rows_home // B
    col_blocks = shard_width * col_count // B
    piece_width = min(B, shard_width)
    per_home = shard_width // piece_width
    per_block = B // piece_width
    sub = piece_width // col_count
    part = per_block * sub
    owners = owned_blocks[0]
    slots = owners.shape[1]

    og = out_grad.T.reshape(per_home, col_count, sub, tok_local).transpose(1, 0, 2, 3)
    og = og.reshape(col_count, per_home * sub, tok_local)
    act = activations.reshape(col_count, tok_local // col_count, activations.shape[1])
    og, act = pl.pallas_call(
        functools.partial(gather_kernel, tok_count, col_count),
        out_shape=[
            jax.ShapeDtypeStruct((tok_count, col_count, per_home * sub, tok_local), bf16),
            jax.ShapeDtypeStruct(
                (tok_count, col_count, tok_local // col_count, rows_home), bf16
            ),
        ],
        in_specs=[ANY, ANY],
        out_specs=[VMEM, VMEM],
        scratch_shapes=[
            pltpu.SemaphoreType.DMA((6, 2, max(col_count, tok_count))),
            pltpu.SemaphoreType.DMA((2,)),
        ],
        compiler_params=pltpu.CompilerParams(
            collective_id=0, has_side_effects=True, vmem_limit_bytes=LIMIT // 4
        ),
    )(og, act)
    og = og.reshape(tok_count, col_count * per_home * sub, tok_local)
    act = act.reshape(tok_count, tok_local, rows_home)

    send = pl.pallas_call(
        functools.partial(
            grad_kernel, slots=slots, row_blocks=row_blocks, col_count=col_count
        ),
        out_shape=jax.ShapeDtypeStruct((col_count, slots, part, B), bf16),
        in_specs=[pl.BlockSpec(memory_space=pltpu.SMEM), VMEM, VMEM],
        out_specs=VMEM,
        scratch_shapes=[pltpu.VMEM((row_blocks, col_blocks, part, B), bf16)],
        compiler_params=pltpu.CompilerParams(vmem_limit_bytes=LIMIT // 2),
    )(owners.reshape(-1), og, act)
    got = lax.all_to_all(send, "col", split_axis=0, concat_axis=0, tiled=True)
    if per_block > 1:
        got = got.reshape(col_count, slots, per_block, sub, B).transpose(2, 0, 3, 1, 4)
        got = got.reshape(col_count, part, slots, B).transpose(0, 2, 1, 3)

    mine = lax.dynamic_index_in_dim(owners, col_index, 0, keepdims=False) >= 0
    square = pl.BlockSpec((1, B, B), lambda s, live: (s, 0, 0))
    pieces = pl.BlockSpec((col_count, 1, part, B), lambda s, live: (0, s, 0, 0))
    back, left_next, right_next = pl.pallas_call(
        slot_kernel,
        out_shape=[
            jax.ShapeDtypeStruct((col_count, slots, part, B), bf16),
            jax.ShapeDtypeStruct((slots, B, B), f32),
            jax.ShapeDtypeStruct((slots, B, B), f32),
        ],
        grid_spec=pltpu.PrefetchScalarGridSpec(
            num_scalar_prefetch=1,
            grid=(slots,),
            in_specs=[pieces, square, square],
            out_specs=[pieces, square, square],
        ),
        compiler_params=pltpu.CompilerParams(vmem_limit_bytes=LIMIT),
    )(mine.astype(jnp.int32), got, gram_left[0, 0], gram_right[0, 0])

    if per_block > 1:
        back = back.transpose(1, 0, 2, 3).reshape(slots, per_block, col_count, sub, B)
        back = back.transpose(2, 0, 1, 3, 4).reshape(col_count, slots, part, B)
    back = lax.all_to_all(back, "col", split_axis=0, concat_axis=0, tiled=True)
    back = back.reshape(col_count * slots, per_block, sub, B)
    home = jnp.arange(col_count * per_home)
    wanted = (tok_index * row_blocks + jnp.arange(row_blocks))[None, :] * col_blocks + (
        home // per_block
    )[:, None]
    match = owners.reshape(-1)[None, None, :] == wanted[:, :, None]
    pick = jnp.argmax(match, axis=2)
    out = back[pick, (home % per_block)[:, None]]
    out = out.reshape(col_count, per_home, row_blocks, sub, B)
    out = lax.all_to_all(out, "col", split_axis=0, concat_axis=0, tiled=True)
    out = pl.pallas_call(
        place_kernel,
        out_shape=jax.ShapeDtypeStruct((rows_home, shard_width), bf16),
        grid=(per_home, row_blocks),
        in_specs=[pl.BlockSpec((col_count, 1, 1, sub, B), lambda h, r: (0, h, r, 0, 0))],
        out_specs=pl.BlockSpec((B, piece_width), lambda h, r: (r, h)),
    )(out)
    return (out, left_next[None, None], right_next[None, None])


def solution(mesh):
    in_specs = (
        P("tok", None),
        P("tok", "col"),
        P("tok", None, None),
        P("tok", "col", None, None, None),
        P("tok", "col", None, None, None),
    )
    out_specs = (
        P("tok", "col"),
        P("tok", "col", None, None, None),
        P("tok", "col", None, None, None),
    )
    return jax.shard_map(
        per_device, mesh=mesh, in_specs=in_specs, out_specs=out_specs, check_vma=False
    )
```

time: 345 us -> 195 us (0.57)
  matrix products: 92.2 us -> 0 us
  Pallas kernels: 0 us -> 86.5 us
  waiting for transfers between devices: 147 us -> 62.7 us
  local copies, waits for them, and re-layouts: 36 us -> 4.87 us
  between operations: 14.2 us -> 0.72 us
  starting transfers between devices: 18.4 us -> 8.92 us
  other arithmetic: 6.52 us -> 1.6 us
    dot_general x9 -> x0, matrix products: 92.2 us -> none  [the longest x6 76.8 us: mm(): jnp.einsum('sij,sjk->sik', a.astype(bf16), b.astype(bf16), preferred_elem...]
    pallas_call x0 -> x4, Pallas kernels: none -> 86.5 us  [the longest x1 52.5 us: per_device(): pl.pallas_call(functools.partial(gather_kernel, tok_count, col_count), ou...]
    all_to_all x2 -> x0, waiting for transfers between devices: 84.3 us -> none  [the longest x1 78.7 us: per_device(): lax.all_to_all(activations, 'tok', split_axis=1, concat_axis=0, tiled=True)]
    unnamed x25 -> x6, local copies, waits for them, and re-layouts: 21.4 us -> 2.16 us
    all_to_all x2 -> x0, starting transfers between devices: 10.2 us -> none  [the longest x1 5.33 us: per_device(): og = lax.all_to_all(og, 'col', split_axis=0, concat_axis=0, tiled=True)]
    reshape x3 -> x0, local copies, waits for them, and re-layouts: 6.47 us -> none  [the longest x2 4.79 us: per_device(): grad = grad.reshape(col_blocks, part, row_blocks, B)]
    convert_element_type x2 -> x1, other arithmetic: 4.35 us -> 0.78 us  [per_device(): mine.astype(jnp.int32)]
  transfers between devices with their start and end apart: 5 -> 2, of which waited for: 4 -> 2; matrix products, arithmetic and copies ran while one was open for 3% -> 1% of each run, Pallas kernels for 0% -> 0%
where the time goes in v2:
time: 195 us
  Pallas kernels  86.5 us (44%)
  waiting for transfers between devices  62.7 us (32%)
  blocking collectives  29.7 us (15%)
  starting transfers between devices  8.92 us (5%)
  local copies, waits for them, and re-layouts  4.87 us (2%)
    pallas_call x1, Pallas kernels, per_device(): pl.pallas_call(functools.partial(gather_kernel, tok_count, col_count), ou...  52.5 us
    all_to_all x1, waiting for transfers between devices, per_device(): got = lax.all_to_all(send, 'col', split_axis=0, concat_axis=0, tiled=True)  31.4 us
    all_to_all x1, waiting for transfers between devices, per_device(): back = lax.all_to_all(back, 'col', split_axis=0, concat_axis=0, tiled=True)  31.2 us
    all_to_all x1, blocking collectives, per_device(): out = lax.all_to_all(out, 'col', split_axis=0, concat_axis=0, tiled=True)  29.7 us
    pallas_call x1, Pallas kernels, per_device(): pl.pallas_call(slot_kernel, out_shape=[jax.ShapeDtypeStruct((col_count, s...  24.8 us
    pallas_call x1, Pallas kernels, per_device(): pl.pallas_call(functools.partial(grad_kernel, slots=slots, row_blocks=row...  5.15 us
    all_to_all x1, starting transfers between devices, per_device(): got = lax.all_to_all(send, 'col', split_axis=0, concat_axis=0, tiled=True)  4.52 us
    all_to_all x1, starting transfers between devices, per_device(): back = lax.all_to_all(back, 'col', split_axis=0, concat_axis=0, tiled=True)  4.39 us
  transfers between devices with their start and end apart: 2, of which 2 were waited for; matrix products, arithmetic and copies ran while one was open for 1% of the time, Pallas kernels for 0%

profile of v2, /device:TPU:0, one launch (start us, length us, event | category | flops | bytes accessed | tf_op | source)
XLA Modules:
  0.0 195.0 jit_solution(7965820216239224479)
XLA Ops:
  0.6 0.0 copy-start
  0.6 0.9 copy.13
  1.5 0.1 reshape_squeeze.3.table
  1.6 1.2 copy.14
  2.9 0.0 copy-done
  2.9 52.5 %shard_map.76 = (bf16[4,8,128,256]{3,2,1,0:T(8,128)(2,1)S(1)}, bf16[4,8,32,1024]{3,2,1,0:T(8,128)(2,1)S(1)}) custom-call(bf16[8,128,256]{2,1,0:T(8,128)(2,1)S(1)} %bitcast.16, bf16[8,32,4096]{2,1,0:T(8,128)(2,1)S(1)} %bitcast.15), custom_call_target="tpu_custom_call" | custom-call | tf_op jit(solution)/shard_map/pallas_call | solution.py:239
  55.4 5.1 %shard_map.77 = bf16[8,5,64,512]{3,2,1,0:T(8,128)(2,1)} custom-call(s32[40]{0:T(128)S(1)} %reshape_squeeze.3.table, bf16[4,1024,256]{2,1,0:T(8,128)(2,1)S(1)} %bitcast.17, bf16[4,256,1024]{2,1,0:T(8,128)(2,1)S(1)} %bitcast.18), custom_call_target="tpu_custom_call" | custom-call | tf_op jit(solution)/shard_map/pallas_call | solution.py:260
  60.6 0.0 copy-start.1
  60.6 4.5 %all-to-all-start = ((bf16[8,5,64,512]{3,2,1,0:T(8,128)(2,1)}), bf16[8,5,64,512]{3,2,1,0:T(8,128)(2,1)}, u32[]{:S(2)}, u32[]{:S(2)}) async-start(bf16[8,5,64,512]{3,2,1,0:T(8,128)(2,1)} %shard_map.77), calls=%async_computation | async-start | bytes 5242880 | tf_op jit(solution)/shard_map/all_to_all | solution.py:270
  65.1 0.0 copy-done.1
  65.1 0.8 fusion.live_ref
  65.9 31.4 %all-to-all-done.got_ref = bf16[8,5,64,512]{3,2,1,0:T(8,128)(2,1)} async-done(((bf16[8,5,64,512]{3,2,1,0:T(8,128)(2,1)}), bf16[8,5,64,512]{3,2,1,0:T(8,128)(2,1)}, u32[]{:S(2)}, u32[]{:S(2)}) %all-to-all-start) | async-done | bytes 2621472 | tf_op jit(solution)/shard_map/all_to_all | solution.py:270
  97.4 24.8 %shard_map.78 = (bf16[8,5,64,512]{3,2,1,0:T(8,128)(2,1)}, f32[5,512,512]{2,1,0:T(8,128)}, f32[5,512,512]{2,1,0:T(8,128)}) custom-call(s32[5]{0:T(128)} %fusion.live_ref, bf16[8,5,64,512]{3,2,1,0:T(8,128)(2,1)} %all-to-all-done.got_ref, f32[5,512,512]{2,1,0:T(8,128)} %bitcast.20, f32[5,512,512]{2,1,0:T(8,128)} %bitcast.21), custom_call_target="tpu_custom_call" | custom-call | tf_op jit(solution)/shard_map/pallas_call | solution.py:278
  122.1 4.4 %all-to-all-start.1 = ((bf16[8,5,64,512]{3,2,1,0:T(8,128)(2,1)}), bf16[8,5,64,512]{3,2,1,0:T(8,128)(2,1)}, u32[]{:S(2)}, u32[]{:S(2)}) async-start(bf16[8,5,64,512]{3,2,1,0:T(8,128)(2,1)} %get-tuple-element.11), calls=%async_computation.1 | async-start | bytes 5242880 | tf_op jit(solution)/shard_map/all_to_all | solution.py:297
  126.5 0.1 iota_add_fusion
  126.6 0.7 iota_reduce_fusion
  127.3 0.1 copy.16
  127.4 0.1 reshape.76
  127.5 31.2 %all-to-all-done.1 = bf16[8,5,64,512]{3,2,1,0:T(8,128)(2,1)} async-done(((bf16[8,5,64,512]{3,2,1,0:T(8,128)(2,1)}), bf16[8,5,64,512]{3,2,1,0:T(8,128)(2,1)}, u32[]{:S(2)}, u32[]{:S(2)}) %all-to-all-start.1) | async-done | bytes 2621472 | tf_op jit(solution)/shard_map/all_to_all | solution.py:297
  158.8 2.4 %gather_fusion = bf16[32,64,512]{2,1,0:T(8,128)(2,1)S(1)} fusion(bf16[40,1,64,512]{3,2,0,1:T(8,128)(2,1)} %bitcast.9, s32[32]{0:T(128)S(1)} %reshape.76), kind=kCustom, calls=%fused_computation | custom fusion | bytes 4194560 | tf_op jit(solution)/shard_map/gather | solution.py:305
  161.2 29.7 %all_to_all.15.in_ref = bf16[8,2,2,64,512]{4,3,2,1,0:T(8,128)(2,1)} all-to-all(bf16[8,2,2,64,512]{4,3,2,1,0:T(8,128)(2,1)S(1)} %bitcast.19), channel_id=1, replica_groups=mesh['tok'=4,'col'=8] {'col'}, dimensions={0} | all-to-all | bytes 4194304 | tf_op jit(solution)/shard_map/all_to_all | solution.py:307
  190.9 4.1 %shard_map.79 = bf16[1024,1024]{1,0:T(8,128)(2,1)} custom-call(bf16[8,2,2,64,512]{4,3,2,1,0:T(8,128)(2,1)} %all_to_all.15.in_ref), custom_call_target="tpu_custom_call" | custom-call | tf_op jit(solution)/shard_map/pallas_call | solution.py:308
  (3 shorter events, 0.0 us)
Async XLA Ops:
  0.6 2.3 %copy-start = (bf16[256,4096]{1,0:T(8,128)(2,1)S(1)}, bf16[256,4096]{1,0:T(8,128)(2,1)}, u32[]{:S(2)}) copy-start(bf16[256,4096]{1,0:T(8,128)(2,1)} %param.5) | copy-start | bytes 6291460
  60.6 4.5 %copy-start.1 = (s32[1,8,5]{1,0,2:T(1,128)S(1)}, s32[1,8,5]{1,0,2:T(1,128)}, u32[]{:S(2)}) copy-start(s32[1,8,5]{1,0,2:T(1,128)} %param.7) | copy-start | bytes 484
  60.6 36.8 %all-to-all-start = ((bf16[8,5,64,512]{3,2,1,0:T(8,128)(2,1)}), bf16[8,5,64,512]{3,2,1,0:T(8,128)(2,1)}, u32[]{:S(2)}, u32[]{:S(2)}) async-start(bf16[8,5,64,512]{3,2,1,0:T(8,128)(2,1)} %shard_map.77), calls=%async_computation | async-start | bytes 5242880 | tf_op jit(solution)/shard_map/all_to_all | solution.py:270
  122.1 36.6 %all-to-all-start.1 = ((bf16[8,5,64,512]{3,2,1,0:T(8,128)(2,1)}), bf16[8,5,64,512]{3,2,1,0:T(8,128)(2,1)}, u32[]{:S(2)}, u32[]{:S(2)}) async-start(bf16[8,5,64,512]{3,2,1,0:T(8,128)(2,1)} %get-tuple-element.11), calls=%async_computation.1 | async-start | bytes 5242880 | tf_op jit(solution)/shard_map/all_to_all | solution.py:297

commit v3 on v2

--- a/solution.py
+++ b/solution.py
@@ -172,8 +172,10 @@
     @pl.loop(0, col_count)
     def _(o):
         for s in range(slots):
-            place = jnp.maximum(table[o * slots + s] - base, 0)
-            send_ref[o, s] = grad[place // col_blocks, lax.rem(place, col_blocks)]
+            owned = table[o * slots + s]
+            place = jnp.maximum(owned - base, 0)
+            piece = grad[place // col_blocks, lax.rem(place, col_blocks)]
+            send_ref[o, s] = jnp.where(owned >= 0, piece, jnp.zeros_like(piece))
 
 
 def root_minus_identity(matrix, diagonal):
@@ -187,19 +189,13 @@
     return (1.25 * e + r - 0.25 * v + mm(v, r)).astype(bf16)
 
 
-def slot_kernel(live_ref, got_ref, left_ref, right_ref, back_ref, left_out, right_out):
-    live = live_ref[pl.program_id(0)] > 0
-    gt = got_ref[...].reshape(B, B)
-    gt = jnp.where(live, gt, jnp.zeros_like(gt))
+def slot_math(gt, left_old, right_old, decay):
     g = gt.T
     rows = lax.broadcasted_iota(jnp.int32, (B, B), 0)
     cols = lax.broadcasted_iota(jnp.int32, (B, B), 1)
     diagonal = rows == cols
-    decay = jnp.where(live, decay_rate, 1.0)
-    left = decay * left_ref[0] + jnp.dot(g, gt, preferred_element_type=f32)
-    right = decay * right_ref[0] + jnp.dot(gt, g, preferred_element_type=f32)
-    left_out[0] = left
-    right_out[0] = right
+    left = decay * left_old + jnp.dot(g, gt, preferred_element_type=f32)
+    right = decay * right_old + jnp.dot(gt, g, preferred_element_type=f32)
     yl = root_minus_identity(left, diagonal)
     yr = root_minus_identity(right, diagonal)
     g32 = gt.astype(f32)
@@ -207,8 +203,137 @@
     shaped = first + mm(first, yl)
     grad_norm = jnp.sqrt(jnp.sum(g32 * g32, keepdims=True) + epsilon)
     shaped_norm = jnp.sqrt(jnp.sum(shaped * shaped, keepdims=True) + epsilon)
-    result = (shaped * (grad_norm / shaped_norm)).astype(bf16)
-    back_ref[...] = result.reshape(back_ref.shape)
+    return (shaped * (grad_norm / shaped_norm)).astype(bf16), left, right
+
+
+def block_kernel(
+    slots,
+    per_home,
+    decay_ref,
+    pick_ref,
+    send_ref,
+    left_ref,
+    right_ref,
+    home_ref,
+    left_out,
+    right_out,
+    grams,
+    got,
+    back,
+    returned,
+    leaving,
+    sems,
+    local_sems,
+):
+    t = lax.axis_index("tok")
+    c = lax.axis_index("col")
+    per_block, col_count = got.shape[1:3]
+    row_blocks = home_ref.shape[2]
+    others = [lax.rem(c + d, col_count) for d in range(1, col_count)]
+
+    barrier = pltpu.get_barrier_semaphore()
+    for other in others:
+        pl.semaphore_signal(barrier, inc=1, device_id=(t, other), device_id_type=MESH)
+
+    def load(side, s):
+        source = (left_ref, right_ref)[side]
+        return pltpu.make_async_copy(source.at[s], grams.at[side, s], local_sems.at[side, s])
+
+    def store(side, s):
+        target = (left_out, right_out)[side]
+        return pltpu.make_async_copy(grams.at[side, s], target.at[s], local_sems.at[side, s])
+
+    def keep(s):
+        return pltpu.make_async_copy(send_ref.at[c, s], got.at[s, :, c], local_sems.at[2, s])
+
+    def keep_back(s):
+        return pltpu.make_async_copy(
+            back.at[s, :, c], returned.at[c * slots + s], local_sems.at[3, s]
+        )
+
+    keep_home = pltpu.make_async_copy(leaving.at[c], home_ref.at[c], local_sems.at[4, 0])
+
+    def remote(src, dst, kind, sent, received, to):
+        return pltpu.make_async_remote_copy(
+            src_ref=src,
+            dst_ref=dst,
+            send_sem=sems.at[kind, 0, sent],
+            recv_sem=sems.at[kind, 1, received],
+            device_id=(t, to),
+            device_id_type=MESH,
+        )
+
+    def out_copy(s, place, to):
+        return remote(send_ref.at[to, s], got.at[s, :, place], s, to, place, to)
+
+    def back_copy(s, place, to):
+        return remote(
+            back.at[s, :, to], returned.at[place * slots + s], slots + s, to, place, to
+        )
+
+    def home_copy(place, to):
+        return remote(leaving.at[to], home_ref.at[place], 2 * slots, to, place, to)
+
+    for s in range(slots):
+        load(0, s).start()
+        load(1, s).start()
+        keep(s).start()
+    pl.semaphore_wait(barrier, col_count - 1)
+
+    @pl.loop(0, slots)
+    def _(s):
+        for other in others:
+            out_copy(s, c, other).start()
+
+    @pl.loop(0, slots)
+    def _(s):
+        keep(s).wait()
+        load(0, s).wait()
+        load(1, s).wait()
+        for other in others:
+            out_copy(s, other, other).wait_recv()
+        result, left, right = slot_math(
+            got[s].reshape(B, B), grams[0, s], grams[1, s], decay_ref[s]
+        )
+        back[s] = result.reshape(back.shape[1:])
+        grams[0, s] = left
+        grams[1, s] = right
+        for other in others:
+            back_copy(s, c, other).start()
+        keep_back(s).start()
+        store(0, s).start()
+        store(1, s).start()
+
+    @pl.loop(0, slots)
+    def _(s):
+        keep_back(s).wait()
+        for other in others:
+            back_copy(s, other, other).wait_recv()
+
+    @pl.loop(0, col_count)
+    def _(h):
+        for p in range(per_home):
+            home = h * per_home + p
+            for r in range(row_blocks):
+                place = pick_ref[(home // per_block) * row_blocks + r]
+                leaving[h, p, r] = returned[place, lax.rem(home, per_block)]
+
+    for other in others:
+        home_copy(c, other).start()
+    keep_home.start()
+
+    @pl.loop(0, slots)
+    def _(s):
+        for other in others:
+            out_copy(s, c, other).wait_send()
+            back_copy(s, c, other).wait_send()
+        store(0, s).wait()
+        store(1, s).wait()
+
+    keep_home.wait()
+    for other in others:
+        home_copy(other, other).wait_recv()
+        home_copy(c, other).wait_send()
 
 
 def place_kernel(in_ref, out_ref):
@@ -267,44 +392,38 @@
         scratch_shapes=[pltpu.VMEM((row_blocks, col_blocks, part, B), bf16)],
         compiler_params=pltpu.CompilerParams(vmem_limit_bytes=LIMIT // 2),
     )(owners.reshape(-1), og, act)
-    got = lax.all_to_all(send, "col", split_axis=0, concat_axis=0, tiled=True)
-    if per_block > 1:
-        got = got.reshape(col_count, slots, per_block, sub, B).transpose(2, 0, 3, 1, 4)
-        got = got.reshape(col_count, part, slots, B).transpose(0, 2, 1, 3)
+    send = send.reshape(col_count, slots, per_block, sub, B)
 
     mine = lax.dynamic_index_in_dim(owners, col_index, 0, keepdims=False) >= 0
-    square = pl.BlockSpec((1, B, B), lambda s, live: (s, 0, 0))
-    pieces = pl.BlockSpec((col_count, 1, part, B), lambda s, live: (0, s, 0, 0))
-    back, left_next, right_next = pl.pallas_call(
-        slot_kernel,
+    decays = jnp.where(mine, decay_rate, 1.0).astype(f32)
+    wanted = (tok_index * row_blocks + jnp.arange(row_blocks))[None, :] * col_blocks + (
+        jnp.arange(col_blocks)
+    )[:, None]
+    match = owners.reshape(-1)[None, None, :] == wanted[:, :, None]
+    pick = jnp.argmax(match, axis=2).astype(jnp.int32).reshape(-1)
+    smem = pl.BlockSpec(memory_space=pltpu.SMEM)
+    out, left_next, right_next = pl.pallas_call(
+        functools.partial(block_kernel, slots, per_home),
         out_shape=[
-            jax.ShapeDtypeStruct((col_count, slots, part, B), bf16),
+            jax.ShapeDtypeStruct((col_count, per_home, row_blocks, sub, B), bf16),
             jax.ShapeDtypeStruct((slots, B, B), f32),
             jax.ShapeDtypeStruct((slots, B, B), f32),
         ],
-        grid_spec=pltpu.PrefetchScalarGridSpec(
-            num_scalar_prefetch=1,
-            grid=(slots,),
-            in_specs=[pieces, square, square],
-            out_specs=[pieces, square, square],
+        in_specs=[smem, smem, ANY, ANY, ANY],
+        out_specs=[VMEM, ANY, ANY],
+        scratch_shapes=[
+            pltpu.VMEM((2, slots, B, B), f32),
+            pltpu.VMEM((slots, per_block, col_count, sub, B), bf16),
+            pltpu.VMEM((slots, per_block, col_count, sub, B), bf16),
+            pltpu.VMEM((col_count * slots, per_block, sub, B), bf16),
+            pltpu.VMEM((col_count, per_home, row_blocks, sub, B), bf16),
+            pltpu.SemaphoreType.DMA((2 * slots + 1, 2, col_count)),
+            pltpu.SemaphoreType.DMA((5, slots)),
+        ],
+        compiler_params=pltpu.CompilerParams(
+            collective_id=1, has_side_effects=True, vmem_limit_bytes=LIMIT
         ),
-        compiler_params=pltpu.CompilerParams(vmem_limit_bytes=LIMIT),
-    )(mine.astype(jnp.int32), got, gram_left[0, 0], gram_right[0, 0])
-
-    if per_block > 1:
-        back = back.transpose(1, 0, 2, 3).reshape(slots, per_block, col_count, sub, B)
-        back = back.transpose(2, 0, 1, 3, 4).reshape(col_count, slots, part, B)
-    back = lax.all_to_all(back, "col", split_axis=0, concat_axis=0, tiled=True)
-    back = back.reshape(col_count * slots, per_block, sub, B)
-    home = jnp.arange(col_count * per_home)
-    wanted = (tok_index * row_blocks + jnp.arange(row_blocks))[None, :] * col_blocks + (
-        home // per_block
-    )[:, None]
-    match = owners.reshape(-1)[None, None, :] == wanted[:, :, None]
-    pick = jnp.argmax(match, axis=2)
-    out = back[pick, (home % per_block)[:, None]]
-    out = out.reshape(col_count, per_home, row_blocks, sub, B)
-    out = lax.all_to_all(out, "col", split_axis=0, concat_axis=0, tiled=True)
+    )(decays, pick, send, gram_left[0, 0], gram_right[0, 0])
     out = pl.pallas_call(
         place_kernel,
         out_shape=jax.ShapeDtypeStruct((rows_home, shard_width), bf16),

time: 195 us -> 166 us (0.85)
  waiting for transfers between devices: 62.7 us -> 0 us
  Pallas kernels: 86.5 us -> 148 us
  blocking collectives: 29.7 us -> 0 us
  local copies, waits for them, and re-layouts: 4.87 us -> 14.2 us
  starting transfers between devices: 8.92 us -> 0 us
    all_to_all x2 -> x0, waiting for transfers between devices: 62.7 us -> none  [the longest x1 31.4 us: per_device(): got = lax.all_to_all(send, 'col', split_axis=0, concat_axis=0, tiled=True)]
    pallas_call x1, Pallas kernels: 24.8 us -> 87.3 us  [per_device(): pl.pallas_call(functools.partial(block_kernel, slots, per_home), out_shap...]
    all_to_all x1 -> x0, blocking collectives: 29.7 us -> none  [per_device(): out = lax.all_to_all(out, 'col', split_axis=0, concat_axis=0, tiled=True)]
    unnamed x6 -> x12, local copies, waits for them, and re-layouts: 2.16 us -> 13.4 us
    all_to_all x2 -> x0, starting transfers between devices: 8.92 us -> none  [the longest x1 4.52 us: per_device(): got = lax.all_to_all(send, 'col', split_axis=0, concat_axis=0, tiled=True)]
    gather x1 -> x0, local copies, waits for them, and re-layouts: 2.42 us -> none  [per_device(): out = back[pick, (home % per_block)[:, None]]]
  transfers between devices with their start and end apart: 2 -> 0, of which waited for: 2 -> 0; matrix products, arithmetic and copies ran while one was open for 1% -> 0% of each run, Pallas kernels for 0% -> 0%
where the time goes in v3:
time: 166 us; the launch traced here: 165 us
  Pallas kernels  148 us (89%)
  local copies, waits for them, and re-layouts  14.2 us (9%)
  other arithmetic  2.2 us (1%)
    pallas_call x1, Pallas kernels, per_device(): pl.pallas_call(functools.partial(block_kernel, slots, per_home), out_shap...  87.3 us
    pallas_call x1, Pallas kernels, per_device(): pl.pallas_call(functools.partial(gather_kernel, tok_count, col_count), ou...  52.5 us
    unnamed x12, local copies, waits for them, and re-layouts  13.4 us
    pallas_call x1, Pallas kernels, per_device(): pl.pallas_call(place_kernel, out_shape=jax.ShapeDtypeStruct((rows_home, s...  4.19 us
    pallas_call x1, Pallas kernels, per_device(): pl.pallas_call(functools.partial(grad_kernel, slots=slots, row_blocks=row...  3.81 us

profile of v3, /device:TPU:0, one launch (start us, length us, event | category | flops | bytes accessed | tf_op | source)
XLA Modules:
  0.0 164.9 jit_solution(4597616117786571856)
XLA Ops:
  0.6 1.4 fusion.decay_ref
  2.0 0.1 iota_add_fusion
  2.1 0.8 copy.13
  2.9 0.1 eq.17.table
  2.9 0.7 iota_reduce_fusion
  3.7 0.1 copy.14
  3.8 0.6 reshape.60.pick_ref
  4.4 1.2 copy.15
  5.7 0.0 copy-start.1
  5.7 1.6 copy-done.1
  7.2 52.5 %shard_map.76 = (bf16[4,8,128,256]{3,2,1,0:T(8,128)(2,1)S(1)}, bf16[4,8,32,1024]{3,2,1,0:T(8,128)(2,1)S(1)}) custom-call(bf16[8,128,256]{2,1,0:T(8,128)(2,1)S(1)} %bitcast.16, bf16[8,32,4096]{2,1,0:T(8,128)(2,1)S(1)} %bitcast.15), custom_call_target="tpu_custom_call" | custom-call | tf_op jit(solution)/shard_map/pallas_call | solution.py:364
  59.7 3.8 %shard_map.77 = bf16[8,5,64,512]{3,2,1,0:T(8,128)(2,1)S(1)} custom-call(s32[40]{0:T(128)S(1)} %eq.17.table, bf16[4,1024,256]{2,1,0:T(8,128)(2,1)S(1)} %bitcast.17, bf16[4,256,1024]{2,1,0:T(8,128)(2,1)S(1)} %bitcast.18), custom_call_target="tpu_custom_call" | custom-call | tf_op jit(solution)/shard_map/pallas_call | solution.py:385
  63.6 0.0 copy-start
  63.6 1.5 copy-done
  65.0 87.3 %shard_map.78 = (bf16[8,2,2,64,512]{4,3,2,1,0:T(8,128)(2,1)}, f32[5,512,512]{2,1,0:T(8,128)}, f32[5,512,512]{2,1,0:T(8,128)}) custom-call(f32[5]{0:T(128)} %fusion.decay_ref, s32[32]{0:T(128)} %reshape.60.pick_ref, bf16[8,5,1,64,512]{4,3,2,1,0:T(8,128)(2,1)} %bitcast.14, f32[5,512,512]{2,1,0:T(8,128)} %bitcast.19, f32[5,512,512]{2,1,0:T(8,128)} %bitcast.20), custom_call_target="tpu_custom_call" | custom-call | tf_op jit(solution)/shard_map/pallas_call | solution.py:405
  152.4 0.0 slice-start
  152.4 4.2 %shard_map.79 = bf16[1024,1024]{1,0:T(8,128)(2,1)} custom-call(bf16[8,2,2,64,512]{4,3,2,1,0:T(8,128)(2,1)} %get-tuple-element.12.in_ref), custom_call_target="tpu_custom_call" | custom-call | tf_op jit(solution)/shard_map/pallas_call | solution.py:427
  156.6 0.0 slice-start.1
  156.6 6.0 %copy.19 = f32[1,1,5,512,512]{4,3,2,1,0:T(8,128)} copy(f32[1,1,5,512,512]{4,3,2,1,0:T(8,128)} %bitcast.24) | data formatting | bytes 10485760
  162.5 0.0 slice-done
  162.5 0.0 slice-done.1
  162.5 2.4 %copy.20 = f32[1,1,5,512,512]{4,3,2,1,0:T(8,128)} copy(f32[1,1,5,512,512]{4,3,2,1,0:T(8,128)S(1)} %bitcast.23) | data formatting | bytes 10485760
  (3 shorter events, 0.0 us)
Async XLA Ops:
  5.7 1.6 copy-start.1
  63.6 1.5 copy-start
  152.4 10.2 %slice-start = ((s8[5242880]{0:T(1024)(128)(4,1)}), s8[1048576]{0:T(1024)(128)(4,1)S(1)}, s32[]{:S(2)}) async-start(s8[5242880]{0:T(1024)(128)(4,1)} %bitcast.21), calls=%async_computation | async-start | bytes 2097152
  156.6 6.0 %slice-start.1 = ((s8[5242880]{0:T(1024)(128)(4,1)}), s8[4194304]{0:T(1024)(128)(4,1)S(1)}, s32[]{:S(2)}) async-start(s8[5242880]{0:T(1024)(128)(4,1)} %bitcast.21), calls=%async_computation.1 | async-start | bytes 8388608

commit v4 on v3

--- a/solution.py
+++ b/solution.py
@@ -15,7 +15,7 @@
 MESH = pl.DeviceIdType.MESH
 VMEM = pl.BlockSpec(memory_space=pltpu.VMEM)
 ANY = pl.BlockSpec(memory_space=pl.ANY)
-LIMIT = 60 * 1024 * 1024
+MIB = 1024 * 1024
 
 
 def mm(a, b):
@@ -150,7 +150,9 @@
             pass_on(origin, -1, 3).wait_send()
 
 
-def grad_kernel(table, og_ref, act_ref, send_ref, grad, *, slots, row_blocks, col_count):
+def grad_kernel(
+    table, og_ref, act_ref, send_ref, pick_ref, decay_ref, grad, *, slots, row_blocks, col_count
+):
     tok_count = og_ref.shape[0]
     col_blocks, part = grad.shape[1:3]
     base = lax.axis_index("tok") * (row_blocks * col_blocks)
@@ -169,6 +171,10 @@
                 blocks, part, B
             )
 
+    mine = lax.axis_index("col") * slots
+    for s in range(slots):
+        decay_ref[s] = jnp.where(table[mine + s] >= 0, f32(decay_rate), f32(1.0))
+
     @pl.loop(0, col_count)
     def _(o):
         for s in range(slots):
@@ -176,6 +182,7 @@
             place = jnp.maximum(owned - base, 0)
             piece = grad[place // col_blocks, lax.rem(place, col_blocks)]
             send_ref[o, s] = jnp.where(owned >= 0, piece, jnp.zeros_like(piece))
+            pick_ref[jnp.where(owned >= 0, place, row_blocks * col_blocks)] = o * slots + s
 
 
 def root_minus_identity(matrix, diagonal):
@@ -217,7 +224,6 @@
     home_ref,
     left_out,
     right_out,
-    grams,
     got,
     back,
     returned,
@@ -229,6 +235,7 @@
     c = lax.axis_index("col")
     per_block, col_count = got.shape[1:3]
     row_blocks = home_ref.shape[2]
+    col_blocks = col_count * per_home // per_block
     others = [lax.rem(c + d, col_count) for d in range(1, col_count)]
 
     barrier = pltpu.get_barrier_semaphore()
@@ -237,11 +244,8 @@
 
     def load(side, s):
         source = (left_ref, right_ref)[side]
-        return pltpu.make_async_copy(source.at[s], grams.at[side, s], local_sems.at[side, s])
-
-    def store(side, s):
         target = (left_out, right_out)[side]
-        return pltpu.make_async_copy(grams.at[side, s], target.at[s], local_sems.at[side, s])
+        return pltpu.make_async_copy(source.at[s], target.at[s], local_sems.at[side, s])
 
     def keep(s):
         return pltpu.make_async_copy(send_ref.at[c, s], got.at[s, :, c], local_sems.at[2, s])
@@ -293,16 +297,14 @@
         for other in others:
             out_copy(s, other, other).wait_recv()
         result, left, right = slot_math(
-            got[s].reshape(B, B), grams[0, s], grams[1, s], decay_ref[s]
+            got[s].reshape(B, B), left_out[s], right_out[s], decay_ref[s]
         )
         back[s] = result.reshape(back.shape[1:])
-        grams[0, s] = left
-        grams[1, s] = right
+        left_out[s] = left
+        right_out[s] = right
         for other in others:
             back_copy(s, c, other).start()
         keep_back(s).start()
-        store(0, s).start()
-        store(1, s).start()
 
     @pl.loop(0, slots)
     def _(s):
@@ -315,7 +317,7 @@
         for p in range(per_home):
             home = h * per_home + p
             for r in range(row_blocks):
-                place = pick_ref[(home // per_block) * row_blocks + r]
+                place = pick_ref[r * col_blocks + home // per_block]
                 leaving[h, p, r] = returned[place, lax.rem(home, per_block)]
 
     for other in others:
@@ -327,8 +329,6 @@
         for other in others:
             out_copy(s, c, other).wait_send()
             back_copy(s, c, other).wait_send()
-        store(0, s).wait()
-        store(1, s).wait()
 
     keep_home.wait()
     for other in others:
@@ -336,9 +336,26 @@
         home_copy(c, other).wait_send()
 
 
-def place_kernel(in_ref, out_ref):
-    width = out_ref.shape[1]
-    out_ref[...] = in_ref[...].reshape(width, B).T
+def place_kernel(in_ref, left_ref, right_ref, out_ref, left_out, right_out, tiles, sems):
+    per_home, row_blocks, _, width = tiles.shape
+    copies = [
+        pltpu.make_async_copy(left_ref, left_out, sems.at[0]),
+        pltpu.make_async_copy(right_ref, right_out, sems.at[1]),
+    ]
+    for copy in copies:
+        copy.start()
+    for h in range(per_home):
+        for r in range(row_blocks):
+            tiles[h, r] = in_ref[:, h, r].reshape(width, B).T
+            copy = pltpu.make_async_copy(
+                tiles.at[h, r],
+                out_ref.at[pl.ds(r * B, B), pl.ds(h * width, width)],
+                sems.at[len(copies)],
+            )
+            copy.start()
+            copies.append(copy)
+    for copy in copies:
+        copy.wait()
 
 
 def per_device(activations, out_grad, owned_blocks, gram_left, gram_right):
@@ -376,32 +393,29 @@
             pltpu.SemaphoreType.DMA((2,)),
         ],
         compiler_params=pltpu.CompilerParams(
-            collective_id=0, has_side_effects=True, vmem_limit_bytes=LIMIT // 4
+            collective_id=0, has_side_effects=True, vmem_limit_bytes=15 * MIB
         ),
     )(og, act)
     og = og.reshape(tok_count, col_count * per_home * sub, tok_local)
     act = act.reshape(tok_count, tok_local, rows_home)
 
-    send = pl.pallas_call(
+    smem = pl.BlockSpec(memory_space=pltpu.SMEM)
+    send, pick, decays = pl.pallas_call(
         functools.partial(
             grad_kernel, slots=slots, row_blocks=row_blocks, col_count=col_count
         ),
-        out_shape=jax.ShapeDtypeStruct((col_count, slots, part, B), bf16),
-        in_specs=[pl.BlockSpec(memory_space=pltpu.SMEM), VMEM, VMEM],
-        out_specs=VMEM,
+        out_shape=[
+            jax.ShapeDtypeStruct((col_count, slots, part, B), bf16),
+            jax.ShapeDtypeStruct((row_blocks * col_blocks + 1,), jnp.int32),
+            jax.ShapeDtypeStruct((slots,), f32),
+        ],
+        in_specs=[smem, VMEM, VMEM],
+        out_specs=[VMEM, smem, smem],
         scratch_shapes=[pltpu.VMEM((row_blocks, col_blocks, part, B), bf16)],
-        compiler_params=pltpu.CompilerParams(vmem_limit_bytes=LIMIT // 2),
+        compiler_params=pltpu.CompilerParams(vmem_limit_bytes=30 * MIB),
     )(owners.reshape(-1), og, act)
     send = send.reshape(col_count, slots, per_block, sub, B)
 
-    mine = lax.dynamic_index_in_dim(owners, col_index, 0, keepdims=False) >= 0
-    decays = jnp.where(mine, decay_rate, 1.0).astype(f32)
-    wanted = (tok_index * row_blocks + jnp.arange(row_blocks))[None, :] * col_blocks + (
-        jnp.arange(col_blocks)
-    )[:, None]
-    match = owners.reshape(-1)[None, None, :] == wanted[:, :, None]
-    pick = jnp.argmax(match, axis=2).astype(jnp.int32).reshape(-1)
-    smem = pl.BlockSpec(memory_space=pltpu.SMEM)
     out, left_next, right_next = pl.pallas_call(
         functools.partial(block_kernel, slots, per_home),
         out_shape=[
@@ -410,9 +424,8 @@
             jax.ShapeDtypeStruct((slots, B, B), f32),
         ],
         in_specs=[smem, smem, ANY, ANY, ANY],
-        out_specs=[VMEM, ANY, ANY],
+        out_specs=[VMEM, VMEM, VMEM],
         scratch_shapes=[
-            pltpu.VMEM((2, slots, B, B), f32),
             pltpu.VMEM((slots, per_block, col_count, sub, B), bf16),
             pltpu.VMEM((slots, per_block, col_count, sub, B), bf16),
             pltpu.VMEM((col_count * slots, per_block, sub, B), bf16),
@@ -421,17 +434,26 @@
             pltpu.SemaphoreType.DMA((5, slots)),
         ],
         compiler_params=pltpu.CompilerParams(
-            collective_id=1, has_side_effects=True, vmem_limit_bytes=LIMIT
+            collective_id=1, has_side_effects=True, vmem_limit_bytes=30 * MIB
         ),
     )(decays, pick, send, gram_left[0, 0], gram_right[0, 0])
-    out = pl.pallas_call(
-        place_kernel,
-        out_shape=jax.ShapeDtypeStruct((rows_home, shard_width), bf16),
-        grid=(per_home, row_blocks),
-        in_specs=[pl.BlockSpec((col_count, 1, 1, sub, B), lambda h, r: (0, h, r, 0, 0))],
-        out_specs=pl.BlockSpec((B, piece_width), lambda h, r: (r, h)),
-    )(out)
-    return (out, left_next[None, None], right_next[None, None])
+    return tuple(
+        pl.pallas_call(
+            place_kernel,
+            out_shape=[
+                jax.ShapeDtypeStruct((rows_home, shard_width), bf16),
+                jax.ShapeDtypeStruct((1, 1, slots, B, B), f32),
+                jax.ShapeDtypeStruct((1, 1, slots, B, B), f32),
+            ],
+            in_specs=[VMEM, VMEM, VMEM],
+            out_specs=[ANY, ANY, ANY],
+            scratch_shapes=[
+                pltpu.VMEM((per_home, row_blocks, B, piece_width), bf16),
+                pltpu.SemaphoreType.DMA((2 + per_home * row_blocks,)),
+            ],
+            compiler_params=pltpu.CompilerParams(vmem_limit_bytes=16 * MIB),
+        )(out, left_next[None, None], right_next[None, None])
+    )
 
 
 def solution(mesh):

time: 166 us -> 153 us (0.922)
  local copies, waits for them, and re-layouts: 14.2 us -> 3.86 us
  other arithmetic: 2.2 us -> 0 us
    unnamed x12 -> x6, local copies, waits for them, and re-layouts: 13.4 us -> 3.75 us
where the time goes in v4:
time: 153 us; the launch traced here: 152 us
  Pallas kernels  147 us (96%)
  local copies, waits for them, and re-layouts  3.86 us (3%)
    pallas_call x1, Pallas kernels, per_device(): pl.pallas_call(functools.partial(block_kernel, slots, per_home), out_shap...  85.7 us
    pallas_call x1, Pallas kernels, per_device(): pl.pallas_call(functools.partial(gather_kernel, tok_count, col_count), ou...  52.5 us
    pallas_call x1, Pallas kernels, per_device(): pl.pallas_call(place_kernel, out_shape=[jax.ShapeDtypeStruct((rows_home,...  4.63 us
    pallas_call x1, Pallas kernels, per_device(): pl.pallas_call(functools.partial(grad_kernel, slots=slots, row_blocks=row...  4.41 us
    unnamed x6, local copies, waits for them, and re-layouts  3.75 us

profile of v4, /device:TPU:0, one launch (start us, length us, event | category | flops | bytes accessed | tf_op | source)
XLA Modules:
  0.0 151.8 jit_solution(13276930695319096798)
XLA Ops:
  0.6 0.8 copy.10
  1.4 0.1 reshape_squeeze.3.table
  1.5 1.2 copy.11
  2.7 0.0 copy-start
  2.8 0.0 copy-start.1
  2.8 1.7 %copy-done.1 = bf16[256,4096]{1,0:T(8,128)(2,1)S(1)} copy-done((bf16[256,4096]{1,0:T(8,128)(2,1)S(1)}, bf16[256,4096]{1,0:T(8,128)(2,1)}, u32[]{:S(2)}) %copy-start.1) | copy-done | bytes 2097176
  4.5 52.5 %shard_map.76 = (bf16[4,8,128,256]{3,2,1,0:T(8,128)(2,1)S(1)}, bf16[4,8,32,1024]{3,2,1,0:T(8,128)(2,1)S(1)}) custom-call(bf16[8,128,256]{2,1,0:T(8,128)(2,1)S(1)} %bitcast.19, bf16[8,32,4096]{2,1,0:T(8,128)(2,1)S(1)} %bitcast.18), custom_call_target="tpu_custom_call" | custom-call | tf_op jit(solution)/shard_map/pallas_call | solution.py:381
  57.0 4.4 %shard_map.77 = (bf16[8,5,64,512]{3,2,1,0:T(8,128)(2,1)S(1)}, s32[33]{0:T(128)S(1)}, f32[5]{0:T(128)S(1)}) custom-call(s32[40]{0:T(128)S(1)} %reshape_squeeze.3.table, bf16[4,1024,256]{2,1,0:T(8,128)(2,1)S(1)} %bitcast.20, bf16[4,256,1024]{2,1,0:T(8,128)(2,1)S(1)} %bitcast.21), custom_call_target="tpu_custom_call" | custom-call | tf_op jit(solution)/shard_map/pallas_call | solution.py:403
  61.4 0.0 copy-done
  61.4 85.7 %shard_map.78 = (bf16[8,2,2,64,512]{4,3,2,1,0:T(8,128)(2,1)S(1)}, f32[5,512,512]{2,1,0:T(8,128)S(1)}, f32[5,512,512]{2,1,0:T(8,128)S(1)}) custom-call(f32[5]{0:T(128)S(1)} %get-tuple-element.13.decay_ref, s32[33]{0:T(128)S(1)} %get-tuple-element.14.pick_ref, bf16[8,5,1,64,512]{4,3,2,1,0:T(8,128)(2,1)S(1)} %bitcast.17, f32[5,512,512]{2,1,0:T(8,128)S(1)} %bitcast.14, ...), custom_call_target="tpu_custom_call" | custom-call | tf_op jit(solution)/shard_map/pallas_call | solution.py:419
  147.1 4.6 %shard_map.79 = (bf16[1024,1024]{1,0:T(8,128)(2,1)}, f32[1,1,5,512,512]{4,3,2,1,0:T(8,128)}, f32[1,1,5,512,512]{4,3,2,1,0:T(8,128)}) custom-call(bf16[8,2,2,64,512]{4,3,2,1,0:T(8,128)(2,1)S(1)} %get-tuple-element.16.in_ref, f32[1,1,5,512,512]{4,3,2,1,0:T(8,128)S(1)} %bitcast.15, f32[1,1,5,512,512]{4,3,2,1,0:T(8,128)S(1)} %bitcast.16), custom_call_target="tpu_custom_call" | custom-call | tf_op jit(solution)/shard_map/pallas_call | solution.py:441
  (1 shorter events, 0.0 us)
Async XLA Ops:
  2.7 58.7 %copy-start = (f32[1,1,5,512,512]{4,3,2,1,0:T(8,128)S(1)}, f32[1,1,5,512,512]{4,3,2,1,0:T(8,128)}, u32[]{:S(2)}) copy-start(f32[1,1,5,512,512]{4,3,2,1,0:T(8,128)} %param.8) | copy-start | bytes 15728644
  2.8 1.7 %copy-start.1 = (bf16[256,4096]{1,0:T(8,128)(2,1)S(1)}, bf16[256,4096]{1,0:T(8,128)(2,1)}, u32[]{:S(2)}) copy-start(bf16[256,4096]{1,0:T(8,128)(2,1)} %param.5) | copy-start | bytes 6291460
